TPU v7x, 256 devices: a whole 4x4x8 slice. The times are simulated.
256 devices in a mesh: depth: 32 (over x, z), views: 8 (over y, core).
Axes of the slice: x: 4, y: 4, z: 8, core: 2. Of those that a mesh axis runs over, the one named last changes fastest.
Arguments:
- density: bfloat16 [512, 128, 128], P('depth'), may hold values from 0.25 to 4
- row_index: int32 [16, 192], replicated, may hold values from 0 to 126, as said below
- row_weight: float32 [16, 192], replicated, may hold values from 0 to 1
- col_index: int32 [16, 192], replicated, may hold values from 0 to 126, as said below
- col_weight: float32 [16, 192], replicated, may hold values from 0 to 1
- assignment: int32 [16], P('views'), may hold values from 0 to 15, each once
- target_image: float32 [16, 36864], P('views'), may hold values from 0.4 to 2
Outputs:
- rendered: float32 [16, 36864], P('views')
- voxel_grad: float32 [512, 128, 128], P(('depth', 'views'))
Inputs may be any that keep to these rules, and one draw needn't show every extreme that they name: `row_index`: along the pixels of each view the indices never fall. `col_index`: along the pixels of each view the indices never fall. `assignment`: each of the 16 views appears once.
All inputs are finite; a program needn't handle non-finite values.
Results may differ from a plain program's by a relative error of at most 0.0046.
Values sent between devices are 32-bit elements; how exact they have to be, the bound alone decides.
A program may use at most 192 MiB of HBM per device.

v0:
```python
import jax
import jax.numpy as jnp
from jax import lax
from jax.sharding import PartitionSpec as P


def resampler(indices, weights, cells):
    places = lax.broadcasted_iota(jnp.int32, indices.shape + (cells,), indices.ndim)
    lower = (places == indices[..., None]).astype(jnp.float32)
    upper = (places == indices[..., None] + 1).astype(jnp.float32)
    return ((1.0 - weights[..., None]) * lower + weights[..., None] * upper).astype(jnp.bfloat16)


def combine(earlier, later):
    return (earlier[0] + earlier[1] * later[0], earlier[1] * later[1])


def on_device(density, row_index, row_weight, col_index, col_weight, assignment, target_image):
    slices = density.shape[0]
    cells = density.shape[1]
    depth_devices = lax.axis_size("depth")
    levels = slices * depth_devices
    step_scale = 1.5 / levels
    rows_matrix = resampler(
        jnp.take(row_index, assignment, axis=0), jnp.take(row_weight, assignment, axis=0), cells
    )
    cols_matrix = resampler(
        jnp.take(col_index, assignment, axis=0), jnp.take(col_weight, assignment, axis=0), cells
    )
    group_views = rows_matrix.shape[0]
    pixels = rows_matrix.shape[1]
    partial_rows = jnp.einsum(
        "via,sab->vsib", rows_matrix, density, preferred_element_type=jnp.float32
    ).astype(jnp.bfloat16)
    samples = jnp.einsum(
        "vsib,vjb->vsij", partial_rows, cols_matrix, preferred_element_type=jnp.float32
    )
    samples = samples.reshape(group_views, slices, pixels * pixels)
    optical = step_scale * samples
    attenuate = jnp.exp(-optical)
    emitted = samples * (1.0 - attenuate)
    running = jnp.cumsum(optical, axis=1)
    through = jnp.exp(-(running - optical))
    inclusive = jnp.cumsum(through * emitted, axis=1)
    block_c = inclusive[:, -1]
    block_t = jnp.exp(-running[:, -1])
    every_c, every_t = (
        lax.all_gather(block_c[None], "depth", axis=0, tiled=True),
        lax.all_gather(block_t[None], "depth", axis=0, tiled=True),
    )
    upto_c, upto_t = lax.associative_scan(combine, (every_c, every_t), axis=0)
    total_c = upto_c[-1]
    lead_c = jnp.concatenate([jnp.zeros_like(upto_c[:1]), upto_c[:-1]], axis=0)
    lead_t = jnp.concatenate([jnp.ones_like(upto_t[:1]), upto_t[:-1]], axis=0)
    position = lax.axis_index("depth")
    before_c = lax.dynamic_index_in_dim(lead_c, position, 0, keepdims=False)
    before_t = lax.dynamic_index_in_dim(lead_t, position, 0, keepdims=False)
    residue = total_c - target_image
    global_through = before_t[:, None, :] * through
    behind = total_c[:, None, :] - (before_c[:, None, :] + before_t[:, None, :] * inclusive)
    grad_samples = (
        levels
        * residue[:, None, :]
        * (global_through * (1.0 - attenuate + optical * attenuate) - step_scale * behind)
    )
    grad_samples = grad_samples.astype(jnp.bfloat16).reshape(group_views, slices, pixels, pixels)
    share = slices // lax.axis_size("views")
    spread = jnp.einsum(
        "vsij,vjb->vsib", grad_samples, cols_matrix, preferred_element_type=jnp.float32
    ).astype(jnp.bfloat16)
    summed = lax.psum(
        jnp.einsum("via,vsib->sab", rows_matrix, spread, preferred_element_type=jnp.float32),
        "views",
    )
    voxel_grad = lax.dynamic_slice_in_dim(summed, lax.axis_index("views") * share, share, 0)
    return (total_c, voxel_grad)


def solution(mesh):
    placed = (P("depth", None, None), P(), P(), P(), P(), P("views"), P("views", None))
    return jax.shard_map(
        on_device,
        mesh=mesh,
        in_specs=placed,
        out_specs=(P("views", None), P(("depth", "views"), None, None)),
        check_vma=False,
    )
```

profile of v0, /device:TPU:1, one launch (start us, length us, event | category | flops | bytes accessed | tf_op | source)
XLA Modules:
  0.0 707.2 jit_solution(7716704007242992718)
XLA Ops:
  69.6 89.6 %all-gather.5.cloned.1.call-done = f32[64,1,36864]{2,1,0:T(1,128)} async-done(((f32[2,1,36864]{2,1,0:T(1,128)}), f32[64,1,36864]{2,1,0:T(1,128)}) %all-gather.5.cloned.1.call-update) | async-done | bytes 9437200 | tf_op jit(solution)/shard_map/all_gather | solution.py:48
  159.2 27.4 %reduce = f32[64,36864]{1,0:T(8,128)} reduce(f32[64,1,36864]{2,1,0:T(1,128)} %all-gather.5.cloned.1.call-done, f32[]{:T(128)} %constant.110), dimensions={1}, to_apply=%all-gather.reduce_sub_computation | reduce | bytes 18874372 | tf_op jit(solution)/shard_map/all_gather | solution.py:48
  186.6 11.4 %reshape.97 = f32[32,2,36864]{2,1,0:T(2,128)} reshape(f32[64,36864]{1,0:T(8,128)} %reduce) | data formatting | bytes 18874368 | tf_op jit(solution)/shard_map/all_gather | solution.py:48
  198.0 64.6 %all-gather.7.cloned.1.call-done = f32[64,1,36864]{2,1,0:T(1,128)} async-done(((f32[2,1,36864]{2,1,0:T(1,128)}), f32[64,1,36864]{2,1,0:T(1,128)}) %all-gather.7.cloned.1.call-update) | async-done | bytes 9437200 | tf_op jit(solution)/shard_map/all_gather | solution.py:49
  262.6 27.3 %reduce.1 = f32[64,36864]{1,0:T(8,128)} reduce(f32[64,1,36864]{2,1,0:T(1,128)} %all-gather.7.cloned.1.call-done, f32[]{:T(128)} %constant.110), dimensions={1}, to_apply=%all-gather.1.reduce_sub_computation | reduce | bytes 18874372 | tf_op jit(solution)/shard_map/all_gather | solution.py:49
  290.0 11.4 %reshape.98 = f32[32,2,36864]{2,1,0:T(2,128)} reshape(f32[64,36864]{1,0:T(8,128)} %reduce.1) | data formatting | bytes 18874368 | tf_op jit(solution)/shard_map/all_gather | solution.py:49
  301.3 9.6 %slice_multiply_fusion = (f32[16,2,36864]{2,1,0:T(2,128)S(1)}, f32[16,2,36864]{2,1,0:T(2,128)S(1)}) fusion(f32[32,2,36864]{2,1,0:T(2,128)} %reshape.98, f32[32,2,36864]{2,1,0:T(2,128)} %reshape.97), kind=kLoop, calls=%fused_computation.9 | loop fusion | flops 3538944 | bytes 28311552 | tf_op jit(solution)/shard_map/mul | solution.py:15
  355.6 8.3 %pad.74 = f32[8,2,36864]{2,1,0:T(2,128)} pad(f32[4,2,36864]{2,1,0:T(2,128)} %pad_maximum_fusion.5, f32[]{:T(128)} %constant.29.clone.1), padding=0_1_1x0_0_0x0_0_0 | pad | bytes 3538948 | tf_op jit(solution)/shard_map/pad | solution.py:51
  363.9 8.3 %pad.75 = f32[8,2,36864]{2,1,0:T(2,128)} pad(f32[4,2,36864]{2,1,0:T(2,128)} %add.159, f32[]{:T(128)} %constant.29.clone.1), padding=1_0_1x0_0_0x0_0_0 | pad | bytes 3538948 | tf_op jit(solution)/shard_map/pad | solution.py:51
  372.2 8.3 %pad.73 = f32[8,2,36864]{2,1,0:T(2,128)} pad(f32[4,2,36864]{2,1,0:T(2,128)} %add.158, f32[]{:T(128)} %constant.29.clone.1), padding=1_0_1x0_0_0x0_0_0 | pad | bytes 3538948 | tf_op jit(solution)/shard_map/pad | solution.py:51
  394.5 9.1 %pad.76 = f32[16,2,36864]{2,1,0:T(2,128)} pad(f32[8,2,36864]{2,1,0:T(2,128)S(1)} %pad_maximum_fusion.2, f32[]{:T(128)} %constant.29.clone.1), padding=0_1_1x0_0_0x0_0_0 | pad | bytes 7077892 | tf_op jit(solution)/shard_map/pad | solution.py:51
  406.3 8.8 %pad.78 = f32[16,2,36864]{2,1,0:T(2,128)} pad(f32[8,2,36864]{2,1,0:T(2,128)S(1)} %pad_maximum_fusion.3, f32[]{:T(128)} %constant.29.clone.1), padding=0_1_1x0_0_0x0_0_0 | pad | bytes 7077892 | tf_op jit(solution)/shard_map/pad | solution.py:51
  415.1 13.8 %pad.79 = f32[16,2,36864]{2,1,0:T(2,128)} pad(f32[8,2,36864]{2,1,0:T(2,128)} %add.162, f32[]{:T(128)} %constant.29.clone.1), padding=1_0_1x0_0_0x0_0_0 | pad | bytes 7077892 | tf_op jit(solution)/shard_map/pad | solution.py:51
  428.9 9.0 %pad.77 = f32[16,2,36864]{2,1,0:T(2,128)} pad(f32[8,2,36864]{2,1,0:T(2,128)S(1)} %copy-done.9, f32[]{:T(128)} %constant.29.clone.1), padding=1_0_1x0_0_0x0_0_0 | pad | bytes 7077892 | tf_op jit(solution)/shard_map/pad | solution.py:51
  437.9 8.9 %add.164 = f32[16,2,36864]{2,1,0:T(2,128)} add(f32[16,2,36864]{2,1,0:T(2,128)} %pad.76, f32[16,2,36864]{2,1,0:T(2,128)} %pad.77) | non-fusion elementwise | flops 1179648 | bytes 14155776 | tf_op jit(solution)/shard_map/add | solution.py:51
  446.8 14.2 %slice_multiply_fusion.1 = (f32[15,2,36864]{2,1,0:T(2,128)}, f32[15,2,36864]{2,1,0:T(2,128)}) fusion(f32[32,2,36864]{2,1,0:T(2,128)} %reshape.98, f32[16,2,36864]{2,1,0:T(2,128)} %pad.79, f32[16,2,36864]{2,1,0:T(2,128)} %pad.78, f32[32,2,36864]{2,1,0:T(2,128)} %reshape.97, f32[16,2,36864]{2,1,0:T(2,128)} %pad.77, f32[16,2,36864]{2,1,0:T(2,128)S(1)} %bitcast.37), kind=kLoop, calls=%fused_computation.14 | loop fusion | flops 5529600 | bytes 35389440 | tf_op jit(solution)/shard_map/mul | solution.py:15
  461.1 8.9 %add.165 = f32[16,2,36864]{2,1,0:T(2,128)} add(f32[16,2,36864]{2,1,0:T(2,128)} %pad.78, f32[16,2,36864]{2,1,0:T(2,128)} %pad.79) | non-fusion elementwise | flops 1179648 | bytes 14155776 | tf_op jit(solution)/shard_map/add | solution.py:51
  475.4 24.2 %pad.108 = f32[31,2,36864]{2,1,0:T(2,128)} pad(f32[16,2,36864]{2,1,0:T(2,128)} %pad_maximum_fusion, f32[]{:T(128)} %constant.29.clone.1), padding=0_0_1x0_0_0x0_0_0 | pad | bytes 13860868 | tf_op jit(solution)/shard_map/slice | solution.py:53
  499.7 24.5 %pad.80 = f32[32,2,36864]{2,1,0:T(2,128)} pad(f32[16,2,36864]{2,1,0:T(2,128)} %pad_maximum_fusion, f32[]{:T(128)} %constant.29.clone.1), padding=0_1_1x0_0_0x0_0_0 | pad | bytes 14155780 | tf_op jit(solution)/shard_map/pad | solution.py:51
  533.1 24.2 %pad.106 = f32[31,2,36864]{2,1,0:T(2,128)} pad(f32[16,2,36864]{2,1,0:T(2,128)} %pad_maximum_fusion.1, f32[]{:T(128)} %constant.29.clone.1), padding=0_0_1x0_0_0x0_0_0 | pad | bytes 13860868 | tf_op jit(solution)/shard_map/slice | solution.py:54
  557.3 24.3 %pad.81 = f32[32,2,36864]{2,1,0:T(2,128)} pad(f32[16,2,36864]{2,1,0:T(2,128)} %add.164, f32[]{:T(128)} %constant.29.clone.1), padding=1_0_1x0_0_0x0_0_0 | pad | bytes 14155780 | tf_op jit(solution)/shard_map/pad | solution.py:51
  581.6 24.3 %pad.154 = f32[32,2,36864]{2,1,0:T(2,128)} pad(f32[16,2,36864]{2,1,0:T(2,128)} %add.165, f32[]{:T(128)} %constant.29.clone.1), padding=1_0_1x0_0_0x0_0_0 | pad | bytes 14155780
  624.8 10.0 %fusion.10 = f32[16,128,128]{1,2,0:T(8,128)} fusion(f32[2,192]{1,0:T(2,128)S(1)} %copy-done.34, s32[2,192]{1,0:T(2,128)S(1)} %copy-done.24, f32[2,192]{1,0:T(2,128)S(1)} %copy-done.32, s32[2,192]{1,0:T(2,128)S(1)} %copy-done.26, f32[2,192]{1,0:T(2,128)S(1)} %copy-done.30, s32[2,192]{1,0:T(2,128)S(1)} %copy-done.20, f32[2,192]{1,0:T(2,128)S(1)} %copy-done.28, ...), kind=kOutput, calls=%fused_computation.30 | convolution fusion | flops 523567104 | bytes 16396288 | tf_op jit(solution)/shard_map/via,vsib->sab/dot_general | solution.py:72
  634.8 63.8 %all-reduce.24.cloned.1.call-done = f32[16,128,128]{1,2,0:T(8,128)} async-done(((f32[16,128,128]{1,2,0:T(8,128)}), f32[16,128,128]{1,2,0:T(8,128)}) %all-reduce.24.cloned.1.call-update) | async-done | bytes 1048592 | tf_op jit(solution)/shard_map/psum | solution.py:71
  (145 shorter events, 158.3 us)
Async XLA Ops:
  7.2 6.7 copy-start
  7.2 152.1 %all-gather.5.cloned.1.call-start = ((), (), s32[]{:S(2)}) async-start(), calls=%async_computation.1 | async-start | bytes 9732096 | tf_op jit(solution)/shard_map/all_gather | solution.py:48
  13.8 10.3 %copy-start.19 = (s32[2,192]{1,0:T(2,128)}, s32[2,192]{1,0:T(2,128)S(1)}, u32[]{:S(2)}) copy-start(s32[2,192]{1,0:T(2,128)S(1)} %get-tuple-element.10) | copy-start | bytes 4612
  13.8 10.3 %copy-start.21 = (s32[2,192]{1,0:T(2,128)}, s32[2,192]{1,0:T(2,128)S(1)}, u32[]{:S(2)}) copy-start(s32[2,192]{1,0:T(2,128)S(1)} %get-tuple-element.11) | copy-start | bytes 4612
  13.8 10.3 %copy-start.23 = (s32[2,192]{1,0:T(2,128)}, s32[2,192]{1,0:T(2,128)S(1)}, u32[]{:S(2)}) copy-start(s32[2,192]{1,0:T(2,128)S(1)} %get-tuple-element.38) | copy-start | bytes 4612
  13.8 10.3 %copy-start.25 = (s32[2,192]{1,0:T(2,128)}, s32[2,192]{1,0:T(2,128)S(1)}, u32[]{:S(2)}) copy-start(s32[2,192]{1,0:T(2,128)S(1)} %get-tuple-element.39) | copy-start | bytes 4612
  13.9 10.2 %copy-start.27 = (f32[2,192]{1,0:T(2,128)}, f32[2,192]{1,0:T(2,128)S(1)}, u32[]{:S(2)}) copy-start(f32[2,192]{1,0:T(2,128)S(1)} %get-tuple-element.8) | copy-start | bytes 4612
  13.9 10.2 %copy-start.29 = (f32[2,192]{1,0:T(2,128)}, f32[2,192]{1,0:T(2,128)S(1)}, u32[]{:S(2)}) copy-start(f32[2,192]{1,0:T(2,128)S(1)} %get-tuple-element.9) | copy-start | bytes 4612
  13.9 10.2 %copy-start.31 = (f32[2,192]{1,0:T(2,128)}, f32[2,192]{1,0:T(2,128)S(1)}, u32[]{:S(2)}) copy-start(f32[2,192]{1,0:T(2,128)S(1)} %get-tuple-element.40) | copy-start | bytes 4612
  13.9 10.2 %copy-start.33 = (f32[2,192]{1,0:T(2,128)}, f32[2,192]{1,0:T(2,128)S(1)}, u32[]{:S(2)}) copy-start(f32[2,192]{1,0:T(2,128)S(1)} %get-tuple-element.41) | copy-start | bytes 4612
  52.9 209.7 %all-gather.7.cloned.1.call-start = ((), (), s32[]{:S(2)}) async-start(), calls=%async_computation.2 | async-start | bytes 9732096 | tf_op jit(solution)/shard_map/all_gather | solution.py:49
  55.7 642.9 %all-reduce.24.cloned.1.call-start = ((), (), s32[]{:S(2)}) async-start(), calls=%async_computation | async-start | bytes 2097152 | tf_op jit(solution)/shard_map/psum | solution.py:71
  321.7 7.3 %copy-start.17 = (f32[1,2,36864]{2,1,0:T(2,128)S(1)}, f32[1,2,36864]{2,1,0:T(2,128)}, u32[]{:S(2)}) copy-start(f32[1,2,36864]{2,1,0:T(2,128)} %get-tuple-element.42) | copy-start | bytes 884740
  337.9 7.0 copy-start.10
  337.9 7.0 copy-start.11
  341.3 5.3 copy-start.16
  345.0 7.9 %copy-start.15 = (f32[1,2,36864]{2,1,0:T(2,128)S(1)}, f32[1,2,36864]{2,1,0:T(2,128)}, u32[]{:S(2)}) copy-start(f32[1,2,36864]{2,1,0:T(2,128)} %slice.237) | copy-start | bytes 884740
  394.5 9.1 %copy-start.13 = (f32[1,2,36864]{2,1,0:T(2,128)S(1)}, f32[1,2,36864]{2,1,0:T(2,128)}, u32[]{:S(2)}) copy-start(f32[1,2,36864]{2,1,0:T(2,128)} %slice.242) | copy-start | bytes 884740
  415.1 13.8 %copy-start.9 = (f32[8,2,36864]{2,1,0:T(2,128)S(1)}, f32[8,2,36864]{2,1,0:T(2,128)}, u32[]{:S(2)}) copy-start(f32[8,2,36864]{2,1,0:T(2,128)} %add.161) | copy-start | bytes 7077892
  428.9 17.9 %slice-start = ((s8[4718592]{0:T(1024)(128)(4,1)}), s8[524288]{0:T(1024)(128)(4,1)S(1)}, s32[]{:S(2)}) async-start(s8[4718592]{0:T(1024)(128)(4,1)} %bitcast.36), calls=%async_computation.3 | async-start | bytes 1048576
  437.9 8.9 %slice-start.1 = ((s8[4718592]{0:T(1024)(128)(4,1)}), s8[4194304]{0:T(1024)(128)(4,1)S(1)}, s32[]{:S(2)}) async-start(s8[4718592]{0:T(1024)(128)(4,1)} %bitcast.36), calls=%async_computation.4 | async-start | bytes 8388608
  461.1 10.1 %copy-start.7 = (f32[15,2,36864]{2,1,0:T(2,128)S(1)}, f32[15,2,36864]{2,1,0:T(2,128)}, u32[]{:S(2)}) copy-start(f32[15,2,36864]{2,1,0:T(2,128)} %get-tuple-element.17) | copy-start | bytes 13271044
  623.9 10.9 %copy-start.12 = (f32[1,2,36864]{2,1,0:T(2,128)}, f32[1,2,36864]{2,1,0:T(2,128)S(1)}, u32[]{:S(2)}) copy-start(f32[1,2,36864]{2,1,0:T(2,128)S(1)} %slice_add_fusion.3) | copy-start | bytes 884740
  624.8 75.5 %copy-start.1 = (bf16[16,128,128]{2,1,0:T(8,128)(2,1)S(1)}, bf16[16,128,128]{2,1,0:T(8,128)(2,1)}, u32[]{:S(2)}) copy-start(bf16[16,128,128]{2,1,0:T(8,128)(2,1)} %param.11) | copy-start | bytes 1572868
  (16 other events, 50.7 us)
Sparse Core Ops, SparseCore 0:
  53.0 106.1 all-gather.4
  162.4 100.1 all-gather.6
  634.9 63.5 all-reduce.23
where the time goes:
time: 719 us; the launch traced here: 707 us
  local copies, waits for them, and re-layouts  265 us (37%)
  waiting for transfers between devices  218 us (30%)
  other arithmetic  195 us (27%)
  between operations  14.7 us (2%)
  matrix products  13.6 us (2%)
    pad x14, local copies, waits for them, and re-layouts, on_device(): upto_c, upto_t = lax.associative_scan(combine, (every_c, every_t), axis=0)  133 us
    all_gather x1, waiting for transfers between devices, on_device(): lax.all_gather(block_c[None], 'depth', axis=0, tiled=True)  89.6 us
    all_gather x1, waiting for transfers between devices, on_device(): lax.all_gather(block_t[None], 'depth', axis=0, tiled=True)  64.6 us
    psum x1, waiting for transfers between devices, on_device(): lax.psum(jnp.einsum('via,vsib->sab', rows_matrix, spread, preferred_eleme...  63.8 us
    add x10, other arithmetic, on_device(): upto_c, upto_t = lax.associative_scan(combine, (every_c, every_t), axis=0)  47.8 us
    mul x7, other arithmetic, combine(): return (earlier[0] + earlier[1] * later[0], earlier[1] * later[1])  37.5 us
    all_gather x1, other arithmetic, on_device(): lax.all_gather(block_c[None], 'depth', axis=0, tiled=True)  27.4 us
    all_gather x1, other arithmetic, on_device(): lax.all_gather(block_t[None], 'depth', axis=0, tiled=True)  27.3 us
  transfers between devices with their start and end apart: 3, of which 3 were waited for; matrix products, arithmetic and copies ran while one was open for 8% of the time, Pallas kernels for 0%

commit v1 on v0

v1 whole, which is shorter than its diff:
```python
import functools

import jax
import jax.numpy as jnp
from jax import lax
from jax.experimental import pallas as pl
from jax.experimental.pallas import tpu as pltpu
from jax.sharding import PartitionSpec as P

MESH = pl.DeviceIdType.MESH
ZDEV = 8
BF = jnp.bfloat16
F32 = jnp.float32


def spread_order(n):
    out = []
    for k in range(1, n // 2 + 1):
        for o in (k, n - k):
            if o not in out and 0 < o < n:
                out.append(o)
    return out


def kernel(
    dims, assign, density, row_index, row_weight, col_index, col_weight, target, image, grad,
    pad_i, pad_w, tall, rows_m, rows_t, cols_m, cols_t, work, goal, gain, shift,
    mine, theirs, local, slab, slabs, back, final, give, got, keep, summed, pieces,
    s1, r1, s2, r2, s3, r3, s4, r4, s5, r5,
):
    nx, nz, ny, levels = dims
    step = 1.5 / levels
    slices, cells = density.shape[0], density.shape[1]
    half = row_index.shape[1] // 2
    pixels = 2 * half
    wide = 2 * pixels
    chunks = 2 * half // 8 // nz
    share = slices // (2 * ny)
    depth, vw = lax.axis_index("depth"), lax.axis_index("views")
    x, z = depth // nz, depth % nz
    y, core = vw // 2, vw % 2

    def at_z(q):
        return (x * nz + q, vw)

    def at_x(q):
        return (q * nz + z, vw)

    def at_y(q):
        return (depth, q * 2 + core)

    partner = (depth, y * 2 + 1 - core)
    z_off, x_off, y_off = spread_order(nz), spread_order(nx), spread_order(ny)

    barrier = pltpu.get_barrier_semaphore()
    for o in z_off:
        pl.semaphore_signal(barrier, inc=1, device_id=at_z((z + o) % nz), device_id_type=MESH)
    for o in x_off:
        pl.semaphore_signal(barrier, inc=1, device_id=at_x((x + o) % nx), device_id_type=MESH)
    for o in y_off:
        pl.semaphore_signal(barrier, inc=1, device_id=at_y((y + o) % ny), device_id_type=MESH)
    pl.semaphore_signal(barrier, inc=1, device_id=partner, device_id_type=MESH)

    pad_i[...] = jnp.full(pad_i.shape, -2, jnp.int32)
    pad_w[...] = jnp.zeros(pad_w.shape, F32)
    for v in range(2):
        a = assign[v]
        pad_i[v : v + 1, 0:pixels] = row_index[pl.ds(a, 1), :]
        pad_w[v : v + 1, 0:pixels] = row_weight[pl.ds(a, 1), :]
        pad_i[2 + v : 3 + v, 0:pixels] = col_index[pl.ds(a, 1), :]
        pad_w[2 + v : 3 + v, 0:pixels] = col_weight[pl.ds(a, 1), :]

    def resampler(row, lanes):
        idx, w = pad_i[row : row + 1, 0:lanes], pad_w[row : row + 1, 0:lanes]
        places = lax.broadcasted_iota(jnp.int32, (cells, lanes), 0)
        zero = jnp.zeros((cells, lanes), F32)
        return jnp.where(places == idx, 1.0 - w, zero) + jnp.where(places == idx + 1, w, zero)

    for v in range(2):
        tall[v] = resampler(v, 2 * cells).T
        ct = resampler(2 + v, wide)
        both = jnp.concatenate([ct, pltpu.roll(ct, pixels, 1)], axis=0)
        cols_m[v] = both.astype(BF)
        cols_t[v] = both.T.astype(BF)
    rows = jnp.concatenate(
        [tall[v, pl.ds(p, half, stride=2), :] for p in range(2) for v in range(2)], axis=0
    )
    rows_m[...] = rows.astype(BF)
    rows_t[...] = rows.T.astype(BF)

    def sample(pair, carry):
        two = jnp.concatenate([density[2 * pair], density[2 * pair + 1]], axis=1)
        part = jnp.dot(rows_m[...], two, preferred_element_type=F32).astype(BF)
        for v in range(2):
            lhs = jnp.concatenate(
                [
                    jnp.concatenate(
                        [
                            part[(2 * p + v) * half : (2 * p + v + 1) * half, s * cells : (s + 1) * cells]
                            for p in range(2)
                        ],
                        axis=1,
                    )
                    for s in range(2)
                ],
                axis=0,
            )
            out = jnp.dot(lhs, cols_m[v], preferred_element_type=F32)
            for s in range(2):
                work[2 * pair + s, v * half : (v + 1) * half, :] = out[s * half : (s + 1) * half]
        return carry

    lax.fori_loop(0, slices // 2, sample, 0)

    def march(tile, carry):
        at = pl.ds(pl.multiple_of(tile * 8, 8), 8)
        through = jnp.ones((8, wide), F32)
        inclusive = jnp.zeros((8, wide), F32)
        for s in range(slices):
            value = work[s, at, :]
            optical = step * value
            att = jnp.exp(-optical)
            gone = 1.0 - att
            inclusive = inclusive + through * (value * gone)
            work[s, at, :] = through * (gone + optical * att) + step * inclusive
            through = through * att
        mine[tile, 0] = inclusive
        mine[tile, 1] = through
        return carry

    pending = []

    def send(src, dst, ssem, rsem, device):
        copy = pltpu.make_async_remote_copy(
            src_ref=src, dst_ref=dst, send_sem=ssem, recv_sem=rsem, device_id=device, device_id_type=MESH
        )
        copy.start()
        pending.append(copy)

    def arrived(dst, rsem):
        pltpu.make_async_remote_copy(
            src_ref=dst, dst_ref=dst, send_sem=rsem, recv_sem=rsem, device_id=partner, device_id_type=MESH
        ).wait_recv()

    for k in range(chunks):
        lax.fori_loop(k * nz, (k + 1) * nz, march, 0)
        if k == 0:
            pl.semaphore_wait(barrier, len(z_off) + len(x_off) + len(y_off) + 1)
        for o in z_off:
            q = (z + o) % nz
            send(mine.at[k * nz + q], theirs.at[k, z], s1.at[k, q], r1.at[k, z], at_z(q))

    for v in range(2):
        for g in range(wide // 128):
            goal[v * half : (v + 1) * half, g * 128 : (g + 1) * 128] = target[
                pl.ds(2 * g + v, half, stride=2 * wide // 128), :
            ]

    def slab_of(k):
        theirs[k, z] = mine[k * nz + z]
        for o in z_off:
            q = (z + o) % nz
            arrived(theirs.at[k, q], r1.at[k, q])
        c = jnp.zeros((8, wide), F32)
        t = jnp.ones((8, wide), F32)
        for q in range(nz):
            local[k, q, 0] = c
            local[k, q, 1] = t
            c = c + t * theirs[k, q, 0]
            t = t * theirs[k, q, 1]
        slab[k, 0] = c
        slab[k, 1] = t
        slabs[k, x, 0] = c
        slabs[k, x, 1] = t
        for o in x_off:
            q = (x + o) % nx
            send(slab.at[k], slabs.at[k, x], s2.at[k, q], r2.at[k, x], at_x(q))

    def lead_of(k):
        for o in x_off:
            q = (x + o) % nx
            arrived(slabs.at[k, q], r2.at[k, q])
        lead_c = jnp.zeros((8, wide), F32)
        lead_t = jnp.ones((8, wide), F32)
        c, t = lead_c, lead_t
        for q in range(nx):
            c = c + t * slabs[k, q, 0]
            t = t * slabs[k, q, 1]
            earlier = q < x
            lead_c = jnp.where(earlier, c, lead_c)
            lead_t = jnp.where(earlier, t, lead_t)
        for q in range(nz):
            back[k, q, 0] = lead_t * local[k, q, 1]
            back[k, q, 1] = c - (lead_c + lead_t * local[k, q, 0])
            back[k, q, 2] = c
        for o in z_off:
            q = (z + o) % nz
            send(back.at[k, q], final.at[k * nz + z], s3.at[k, q], r3.at[k, z], at_z(q))
        final[k * nz + z] = back[k, z]

    for k in range(chunks + 1):
        if k < chunks:
            slab_of(k)
        if k >= 1:
            lead_of(k - 1)

    for k in range(chunks):
        for o in z_off:
            q = (z + o) % nz
            arrived(final.at[k * nz + q], r3.at[k, q])
    per = half // 8
    for v in range(2):
        at = slice(v * half, (v + 1) * half)
        residue = levels * (final[v * per : (v + 1) * per, 2].reshape(half, wide) - goal[at])
        gain[at] = residue * final[v * per : (v + 1) * per, 0].reshape(half, wide)
        shift[at] = step * residue * final[v * per : (v + 1) * per, 1].reshape(half, wide)

    def terms(first):
        g = [(gain[...] * work[first + s] - shift[...]).astype(BF) for s in range(2)]
        spread = [
            jnp.dot(
                jnp.concatenate([g[s][v * half : (v + 1) * half] for s in range(2)], axis=0),
                cols_t[v],
                preferred_element_type=F32,
            ).astype(BF)
            for v in range(2)
        ]
        stack = jnp.concatenate(
            [
                jnp.concatenate(
                    [
                        spread[v][s * half : (s + 1) * half, p * cells : (p + 1) * cells]
                        for p in range(2)
                        for v in range(2)
                    ],
                    axis=0,
                )
                for s in range(2)
            ],
            axis=1,
        )
        out = jnp.dot(rows_t[...], stack, preferred_element_type=F32)
        return [out[:, s * cells : (s + 1) * cells] for s in range(2)]

    def merge(o):
        q = (y + o) % ny
        arrived(got.at[q], r4.at[q])
        summed[q] = keep[q] + got[q]
        if o:
            send(summed.at[q], pieces.at[y], s5.at[q], r5.at[y], at_y(q))

    order = y_off[::-1] + [0]
    for n, o in enumerate(order):
        q = (y + o) % ny
        for i in range(0, share, 2):
            out = terms((2 * q + 1 - core) * share + i)
            for s in range(2):
                give[q, i + s] = out[s]
        send(give.at[q], got.at[q], s4.at[q], r4.at[q], partner)
        for i in range(0, share, 2):
            out = terms((2 * q + core) * share + i)
            for s in range(2):
                keep[q, i + s] = out[s]
        if n:
            merge(order[n - 1])
    merge(0)

    for v in range(2):
        for g in range(wide // 128):
            image[pl.ds(2 * g + v, half, stride=2 * wide // 128), :] = final[
                v * per : (v + 1) * per, 2, :, g * 128 : (g + 1) * 128
            ].reshape(half, 128)

    total = summed[y]
    for o in y_off:
        q = (y + o) % ny
        arrived(pieces.at[q], r5.at[q])
        total = total + pieces[q]
    grad[...] = total
    for copy in pending:
        copy.wait_send()


def on_device(nx, nz, ny, density, row_index, row_weight, col_index, col_weight, assignment, target_image):
    slices, cells = density.shape[0], density.shape[1]
    views, flat = target_image.shape
    pixels = row_index.shape[1]
    wide, tiles = 2 * pixels, flat * views // (8 * 2 * pixels)
    chunks = tiles // nz
    share = slices // (2 * ny)
    lines = flat // 128
    vm = pl.BlockSpec(memory_space=pltpu.VMEM)
    dma = pltpu.SemaphoreType.DMA
    image, grad = pl.pallas_call(
        functools.partial(kernel, (nx, nz, ny, slices * nx * nz)),
        out_shape=(
            jax.ShapeDtypeStruct((views * lines, 128), F32),
            jax.ShapeDtypeStruct((share, cells, cells), F32),
        ),
        in_specs=[pl.BlockSpec(memory_space=pltpu.SMEM)] + [vm] * 6,
        out_specs=(vm, vm),
        scratch_shapes=[
            pltpu.VMEM((8, wide), jnp.int32),
            pltpu.VMEM((8, wide), F32),
            pltpu.VMEM((2, 2 * cells, cells), F32),
            pltpu.VMEM((wide, cells), BF),
            pltpu.VMEM((cells, wide), BF),
            pltpu.VMEM((2, 2 * cells, wide), BF),
            pltpu.VMEM((2, wide, 2 * cells), BF),
            pltpu.VMEM((slices, pixels, wide), F32),
            pltpu.VMEM((pixels, wide), F32),
            pltpu.VMEM((pixels, wide), F32),
            pltpu.VMEM((pixels, wide), F32),
            pltpu.VMEM((tiles, 2, 8, wide), F32),
            pltpu.VMEM((chunks, nz, 2, 8, wide), F32),
            pltpu.VMEM((chunks, nz, 2, 8, wide), F32),
            pltpu.VMEM((chunks, 2, 8, wide), F32),
            pltpu.VMEM((chunks, nx, 2, 8, wide), F32),
            pltpu.VMEM((chunks, nz, 3, 8, wide), F32),
            pltpu.VMEM((tiles, 3, 8, wide), F32),
            pltpu.VMEM((ny, share, cells, cells), F32),
            pltpu.VMEM((ny, share, cells, cells), F32),
            pltpu.VMEM((ny, share, cells, cells), F32),
            pltpu.VMEM((ny, share, cells, cells), F32),
            pltpu.VMEM((ny, share, cells, cells), F32),
            dma((chunks, nz)), dma((chunks, nz)),
            dma((chunks, nx)), dma((chunks, nx)),
            dma((chunks, nz)), dma((chunks, nz)),
            dma((ny,)), dma((ny,)),
            dma((ny,)), dma((ny,)),
        ],
        compiler_params=pltpu.CompilerParams(
            collective_id=0, has_side_effects=True, vmem_limit_bytes=48 << 20
        ),
    )(
        assignment, density, row_index, row_weight, col_index, col_weight,
        target_image.reshape(views, lines, 128).transpose(1, 0, 2).reshape(views * lines, 128),
    )
    return image.reshape(lines, views, 128).transpose(1, 0, 2).reshape(views, flat), grad


def solution(mesh, nz=ZDEV):
    placed = (P("depth", None, None), P(), P(), P(), P(), P("views"), P("views", None))
    nx, ny = mesh.shape["depth"] // nz, mesh.shape["views"] // 2
    return jax.shard_map(
        functools.partial(on_device, nx, nz, ny),
        mesh=mesh,
        in_specs=placed,
        out_specs=(P("views", None), P(("depth", "views"), None, None)),
        check_vma=False,
    )
```

time: 719 us -> 66.6 us (0.09); the launches traced: 707 us -> 66.2 us
  local copies, waits for them, and re-layouts: 265 us -> 6.89 us
  waiting for transfers between devices: 218 us -> 0 us
  other arithmetic: 195 us -> 0 us
  Pallas kernels: 0 us -> 58.6 us
  between operations: 14.7 us -> 0.66 us
  matrix products: 13.6 us -> 0 us
    all_gather x2 -> x0, waiting for transfers between devices: 154 us -> none  [the longest x1 89.6 us: on_device(): lax.all_gather(block_c[None], 'depth', axis=0, tiled=True)]
    pad x14 -> x0, local copies, waits for them, and re-layouts: 133 us -> none  [on_device(): upto_c, upto_t = lax.associative_scan(combine, (every_c, every_t), axis=0)]
    psum x1 -> x0, waiting for transfers between devices: 63.8 us -> none  [on_device(): lax.psum(jnp.einsum('via,vsib->sab', rows_matrix, spread, preferred_eleme...]
    pallas_call x0 -> x1, Pallas kernels: none -> 58.6 us  [on_device(): pl.pallas_call(functools.partial(kernel, (nx, nz, ny, slices * nx * nz)),...]
    slice x11 -> x0, local copies, waits for them, and re-layouts: 57.1 us -> none  [the longest x1 24.2 us: on_device(): lead_c = jnp.concatenate([jnp.zeros_like(upto_c[:1]), upto_c[:-1]], axis=0)]
    all_gather x2 -> x0, other arithmetic: 54.7 us -> none  [the longest x1 27.4 us: on_device(): lax.all_gather(block_c[None], 'depth', axis=0, tiled=True)]
    mul x10 -> x0, other arithmetic: 49.9 us -> none  [the longest x7 37.5 us: combine(): return (earlier[0] + earlier[1] * later[0], earlier[1] * later[1])]
    add x11 -> x0, other arithmetic: 47.9 us -> none  [the longest x10 47.8 us: on_device(): upto_c, upto_t = lax.associative_scan(combine, (every_c, every_t), axis=0)]
  transfers between devices with their start and end apart: 3 -> 0, of which waited for: 3 -> 0; matrix products, arithmetic and copies ran while one was open for 8% -> 0% of each run, Pallas kernels for 0% -> 0%
where the time goes in v1:
time: 66.6 us; the launch traced here: 66.2 us
  Pallas kernels  58.6 us (88%)
  local copies, waits for them, and re-layouts  6.89 us (10%)
    pallas_call x1, Pallas kernels, on_device(): pl.pallas_call(functools.partial(kernel, (nx, nz, ny, slices * nx * nz)),...  58.6 us
    unnamed x16, local copies, waits for them, and re-layouts  6.89 us

profile of v1, /device:TPU:1, one launch (start us, length us, event | category | flops | bytes accessed | tf_op | source)
XLA Modules:
  0.0 66.2 jit_solution(16575087036697693614)
XLA Ops:
  0.6 0.0 copy-start.6
  0.6 0.6 copy-done.6
  1.3 0.0 copy-start
  1.3 1.0 %copy-done = bf16[16,128,128]{2,1,0:T(8,128)(2,1)S(1)} copy-done((bf16[16,128,128]{2,1,0:T(8,128)(2,1)S(1)}, bf16[16,128,128]{2,1,0:T(8,128)(2,1)}, u32[]{:S(2)}) %copy-start) | copy-done | bytes 524312
  2.3 0.0 copy-start.1
  2.3 1.0 %copy-done.1 = f32[2,36864]{1,0:T(2,128)S(1)} copy-done((f32[2,36864]{1,0:T(2,128)S(1)}, f32[2,36864]{1,0:T(2,128)}, u32[]{:S(2)}) %copy-start.1) | copy-done | bytes 294936
  3.3 0.0 copy-start.2
  3.3 0.7 %copy-done.2 = s32[16,192]{1,0:T(8,128)S(1)} copy-done((s32[16,192]{1,0:T(8,128)S(1)}, s32[16,192]{1,0:T(8,128)}, u32[]{:S(2)}) %copy-start.2) | copy-done | bytes 12312
  4.0 0.0 copy-start.3
  4.0 0.7 %copy-done.3 = f32[16,192]{1,0:T(8,128)S(1)} copy-done((f32[16,192]{1,0:T(8,128)S(1)}, f32[16,192]{1,0:T(8,128)}, u32[]{:S(2)}) %copy-start.3) | copy-done | bytes 12312
  4.7 0.0 copy-start.4
  4.7 0.7 %copy-done.4 = s32[16,192]{1,0:T(8,128)S(1)} copy-done((s32[16,192]{1,0:T(8,128)S(1)}, s32[16,192]{1,0:T(8,128)}, u32[]{:S(2)}) %copy-start.4) | copy-done | bytes 12312
  5.4 0.0 copy-start.5
  5.4 0.7 %copy-done.5 = f32[16,192]{1,0:T(8,128)S(1)} copy-done((f32[16,192]{1,0:T(8,128)S(1)}, f32[16,192]{1,0:T(8,128)}, u32[]{:S(2)}) %copy-start.5) | copy-done | bytes 12312
  6.2 58.6 %shard_map.86 = (f32[576,128]{1,0:T(8,128)S(1)}, f32[2,128,128]{2,1,0:T(8,128)S(1)}) custom-call(s32[2]{0:T(128)S(1)} %copy-done.6, bf16[16,128,128]{2,1,0:T(8,128)(2,1)S(1)} %copy-done, s32[16,192]{1,0:T(8,128)S(1)} %copy-done.2, f32[16,192]{1,0:T(8,128)S(1)} %copy-done.3, s32[16,192]{1,0:T(8,128)S(1)} %copy-done.4, f32[16,192]{1,0:T(8,128)S(1)} %copy-done.5, ...), custom_call_target="tpu_custom_call" | custom-call | tf_op jit(solution)/shard_map/pallas_call | solution.py:294
  64.8 0.7 %copy.13 = f32[2,36864]{1,0:T(2,128)} copy(f32[2,36864]{1,0:T(2,128)S(1)} %bitcast.11) | data formatting | bytes 589824
  65.5 0.7 copy.14
Async XLA Ops:
  0.6 0.7 copy-start.6
  1.3 1.0 %copy-start = (bf16[16,128,128]{2,1,0:T(8,128)(2,1)S(1)}, bf16[16,128,128]{2,1,0:T(8,128)(2,1)}, u32[]{:S(2)}) copy-start(bf16[16,128,128]{2,1,0:T(8,128)(2,1)} %density.1) | copy-start | bytes 1572868
  2.3 1.0 %copy-start.1 = (f32[2,36864]{1,0:T(2,128)S(1)}, f32[2,36864]{1,0:T(2,128)}, u32[]{:S(2)}) copy-start(f32[2,36864]{1,0:T(2,128)} %param.13) | copy-start | bytes 884740
  3.3 0.7 %copy-start.2 = (s32[16,192]{1,0:T(8,128)S(1)}, s32[16,192]{1,0:T(8,128)}, u32[]{:S(2)}) copy-start(s32[16,192]{1,0:T(8,128)} %row_index.1) | copy-start | bytes 36868
  4.0 0.7 %copy-start.3 = (f32[16,192]{1,0:T(8,128)S(1)}, f32[16,192]{1,0:T(8,128)}, u32[]{:S(2)}) copy-start(f32[16,192]{1,0:T(8,128)} %row_weight.1) | copy-start | bytes 36868
  4.7 0.7 %copy-start.4 = (s32[16,192]{1,0:T(8,128)S(1)}, s32[16,192]{1,0:T(8,128)}, u32[]{:S(2)}) copy-start(s32[16,192]{1,0:T(8,128)} %col_index.1) | copy-start | bytes 36868
  5.4 0.7 %copy-start.5 = (f32[16,192]{1,0:T(8,128)S(1)}, f32[16,192]{1,0:T(8,128)}, u32[]{:S(2)}) copy-start(f32[16,192]{1,0:T(8,128)} %col_weight.1) | copy-start | bytes 36868

commit v2 on v1

v2 whole, which is shorter than its diff:
```python
import functools

import jax
import jax.numpy as jnp
from jax import lax
from jax.experimental import pallas as pl
from jax.experimental.pallas import tpu as pltpu
from jax.sharding import PartitionSpec as P

MESH = pl.DeviceIdType.MESH
ZDEV = 8
BF = jnp.bfloat16
F32 = jnp.float32
LOG2E = 1.4426950408889634


def spread_order(n):
    out = []
    for k in range(1, n // 2 + 1):
        for o in (k, n - k):
            if o not in out and 0 < o < n:
                out.append(o)
    return out


def kernel(
    dims, *refs
):
    (
    assign_h, density_h, row_index_h, row_weight_h, col_index_h, col_weight_h, target_h, image, grad,
    assign, density, row_index, row_weight, col_index, col_weight, target, loads,
    pad_i, pad_w, tall, rows_m, rows_t, cols_m, cols_t, crossed, work, goal, gain, shift,
    mine, theirs, local, slab, slabs, back, final, totals, part, give, got, keep, summed, pieces,
    s1, r1, s2, r2, s3, r3, s4, r4, s5, r5, s6, r6, s7, r7,
    ) = refs
    nx, nz, ny, levels = dims
    step = 1.5 / levels
    slices, cells = density.shape[0], density.shape[1]
    half = row_index.shape[1] // 2
    pixels = 2 * half
    wide = 2 * pixels
    chunks = 2 * half // 8 // nz
    share = slices // (2 * ny)
    depth, vw = lax.axis_index("depth"), lax.axis_index("views")
    x, z = depth // nz, depth % nz
    y, core = vw // 2, vw % 2

    def at_z(q):
        return (x * nz + q, vw)

    def at_x(q):
        return (q * nz + z, vw)

    def at_y(q):
        return (depth, q * 2 + core)

    partner = (depth, y * 2 + 1 - core)
    z_off, x_off, y_off = spread_order(nz), spread_order(nx), spread_order(ny)

    fetch = [
        pltpu.make_async_copy(src, dst, loads.at[n])
        for n, (src, dst) in enumerate(
            [
                (assign_h, assign), (row_index_h, row_index), (row_weight_h, row_weight),
                (col_index_h, col_index), (col_weight_h, col_weight),
                (density_h, density), (target_h, target),
            ]
        )
    ]
    for copy in fetch:
        copy.start()

    barrier = pltpu.get_barrier_semaphore()
    for o in z_off:
        pl.semaphore_signal(barrier, inc=1, device_id=at_z((z + o) % nz), device_id_type=MESH)
    for o in x_off:
        pl.semaphore_signal(barrier, inc=1, device_id=at_x((x + o) % nx), device_id_type=MESH)
    for o in y_off:
        pl.semaphore_signal(barrier, inc=1, device_id=at_y((y + o) % ny), device_id_type=MESH)
    pl.semaphore_signal(barrier, inc=1, device_id=partner, device_id_type=MESH)

    for copy in fetch[:5]:
        copy.wait()
    pad_i[...] = jnp.full(pad_i.shape, -2, jnp.int32)
    pad_w[...] = jnp.zeros(pad_w.shape, F32)
    for v in range(2):
        a = assign[v]
        pad_i[v : v + 1, 0:pixels] = row_index[pl.ds(a, 1), :]
        pad_w[v : v + 1, 0:pixels] = row_weight[pl.ds(a, 1), :]
        pad_i[2 + v : 3 + v, 0:pixels] = col_index[pl.ds(a, 1), :]
        pad_w[2 + v : 3 + v, 0:pixels] = col_weight[pl.ds(a, 1), :]

    def resampler(row, lanes):
        idx, w = pad_i[row : row + 1, 0:lanes], pad_w[row : row + 1, 0:lanes]
        places = lax.broadcasted_iota(jnp.int32, (cells, lanes), 0)
        zero = jnp.zeros((cells, lanes), F32)
        return jnp.where(places == idx, 1.0 - w, zero) + jnp.where(places == idx + 1, w, zero)

    for v in range(2):
        tall[v] = resampler(v, 2 * cells).T
        ct = resampler(2 + v, wide)
        both = jnp.concatenate([ct, pltpu.roll(ct, pixels, 1)], axis=0)
        cols_m[v] = both.astype(BF)
        cols_t[v] = both.T.astype(BF)
    rows = jnp.concatenate(
        [tall[v, pl.ds(p, half, stride=2), :] for p in range(2) for v in range(2)], axis=0
    )
    rows_m[...] = rows.astype(BF)
    tall_rows = 8 * nz
    for k in range(chunks):
        at = k * tall_rows
        both = jnp.concatenate([rows[p * pixels + at : p * pixels + at + tall_rows] for p in range(2)], axis=0)
        rows_t[k] = both.T.astype(BF)

    def views_in(k):
        out = []
        for v in range(2):
            lo, hi = max(k * tall_rows, v * half), min((k + 1) * tall_rows, (v + 1) * half)
            if lo < hi:
                out.append((v, lo - k * tall_rows, hi - lo))
        return out

    def sample(k):
        at = k * tall_rows
        lhs = jnp.concatenate(
            [rows_m[p * pixels + at : p * pixels + at + tall_rows, :] for p in range(2)], axis=0
        )
        for pair in range(slices // 2):
            two = jnp.concatenate([density[2 * pair], density[2 * pair + 1]], axis=1)
            out = jnp.dot(lhs, two, preferred_element_type=F32).astype(BF)
            for s in range(2):
                cut = out[:, s * cells : (s + 1) * cells]
                crossed[2 * pair + s] = jnp.concatenate([cut[:tall_rows], cut[tall_rows:]], axis=1)
        for v, first, n in views_in(k):
            out = jnp.dot(
                crossed[:, first : first + n, :].reshape(slices * n, 2 * cells),
                cols_m[v],
                preferred_element_type=F32,
            )
            work[:, at + first : at + first + n, :] = out.reshape(slices, n, wide)

    def march(tile, carry):
        at = pl.ds(pl.multiple_of(tile * 8, 8), 8)
        through = jnp.ones((8, wide), F32)
        inclusive = jnp.zeros((8, wide), F32)
        for s in range(slices):
            value = work[s, at, :]
            optical = step * value
            att = jnp.exp2(value * (-step * LOG2E))
            gone = 1.0 - att
            inclusive = inclusive + through * (optical * gone)
            work[s, at, :] = through * (gone + optical * att) + inclusive
            through = through * att
        mine[tile, 0] = inclusive * (1.0 / step)
        mine[tile, 1] = through
        return carry

    pending = []

    def send(src, dst, ssem, rsem, device):
        copy = pltpu.make_async_remote_copy(
            src_ref=src, dst_ref=dst, send_sem=ssem, recv_sem=rsem, device_id=device, device_id_type=MESH
        )
        copy.start()
        return copy

    def arrived(dst, rsem):
        pltpu.make_async_remote_copy(
            src_ref=dst, dst_ref=dst, send_sem=rsem, recv_sem=rsem, device_id=partner, device_id_type=MESH
        ).wait_recv()

    fetch[5].wait()
    for k in range(chunks):
        sample(k)
        lax.fori_loop(k * nz, (k + 1) * nz, march, 0)
        if k == 0:
            pl.semaphore_wait(barrier, len(z_off) + len(x_off) + len(y_off) + 1)
        for o in z_off:
            q = (z + o) % nz
            pending.append(send(mine.at[k * nz + q], theirs.at[k, z], s1.at[k, q], r1.at[k, z], at_z(q)))

    fetch[6].wait()
    groups = wide // 128
    for v in range(2):
        for g in range(groups):
            goal[v * half : (v + 1) * half, g * 128 : (g + 1) * 128] = target[
                pl.ds(2 * g + v, half, stride=2 * groups), :
            ]

    def slab_of(k):
        theirs[k, z] = mine[k * nz + z]
        for o in z_off:
            q = (z + o) % nz
            arrived(theirs.at[k, q], r1.at[k, q])
        c = jnp.zeros((8, wide), F32)
        t = jnp.ones((8, wide), F32)
        for q in range(nz):
            local[k, q, 0] = c
            local[k, q, 1] = t
            c = c + t * theirs[k, q, 0]
            t = t * theirs[k, q, 1]
        slab[k, 0] = c
        slab[k, 1] = t
        slabs[k, x, 0] = c
        slabs[k, x, 1] = t
        for o in x_off:
            q = (x + o) % nx
            pending.append(send(slab.at[k], slabs.at[k, x], s2.at[k, q], r2.at[k, x], at_x(q)))

    def lead_of(k):
        for o in x_off:
            q = (x + o) % nx
            arrived(slabs.at[k, q], r2.at[k, q])
        lead_c = jnp.zeros((8, wide), F32)
        lead_t = jnp.ones((8, wide), F32)
        c, t = lead_c, lead_t
        for q in range(nx):
            c = c + t * slabs[k, q, 0]
            t = t * slabs[k, q, 1]
            earlier = q < x
            lead_c = jnp.where(earlier, c, lead_c)
            lead_t = jnp.where(earlier, t, lead_t)
        own = k * nz + z
        for g in range(groups):

            @pl.when(x == g % nx)
            def _():
                totals[g, own] = c[:, g * 128 : (g + 1) * 128]
                for o in z_off:
                    q = (z + o) % nz
                    send(totals.at[g, own], totals.at[g, own], s6.at[k, g, q], r6.at[k, g, z], at_z(q))

        for q in range(nz):
            back[k, q, 0] = lead_t * local[k, q, 1]
            back[k, q, 1] = c - (lead_c + lead_t * local[k, q, 0])
        for o in z_off:
            q = (z + o) % nz
            pending.append(send(back.at[k, q], final.at[own], s3.at[k, q], r3.at[k, z], at_z(q)))
        final[own] = back[k, z]

    def share_of(k):
        for g in range(groups):

            @pl.when(x == g % nx)
            def _():
                for o in z_off:
                    q = (z + o) % nz
                    arrived(totals.at[g, k * nz + q], r6.at[k, g, q])
                for o in x_off:
                    q = (x + o) % nx
                    tiles = totals.at[g, k * nz : (k + 1) * nz]
                    send(tiles, tiles, s7.at[k, g, q], r7.at[k, g], at_x(q))

    def sent_totals(k):
        for g in range(groups):

            @pl.when(x == g % nx)
            def _():
                one = totals.at[g, k * nz + z]
                tiles = totals.at[g, k * nz : (k + 1) * nz]
                for o in z_off:
                    q = (z + o) % nz
                    pltpu.make_async_remote_copy(
                        src_ref=one, dst_ref=one, send_sem=s6.at[k, g, q], recv_sem=r6.at[k, g, z],
                        device_id=at_z(q), device_id_type=MESH,
                    ).wait_send()
                for o in x_off:
                    q = (x + o) % nx
                    pltpu.make_async_remote_copy(
                        src_ref=tiles, dst_ref=tiles, send_sem=s7.at[k, g, q], recv_sem=r7.at[k, g],
                        device_id=at_x(q), device_id_type=MESH,
                    ).wait_send()

    def weigh(k):
        for o in z_off:
            q = (z + o) % nz
            arrived(final.at[k * nz + q], r3.at[k, q])
        for g in range(groups):

            @pl.when(x != g % nx)
            def _():
                arrived(totals.at[g, k * nz : (k + 1) * nz], r7.at[k, g])

        at = slice(k * tall_rows, (k + 1) * tall_rows)
        tiles = slice(k * nz, (k + 1) * nz)
        total = jnp.concatenate([totals[g, tiles].reshape(tall_rows, 128) for g in range(groups)], axis=1)
        residue = levels * (total - goal[at])
        gain[at] = residue * final[tiles, 0].reshape(tall_rows, wide)
        shift[at] = step * residue * final[tiles, 1].reshape(tall_rows, wide)

    def terms(k, first, count):
        at = slice(k * tall_rows, (k + 1) * tall_rows)
        g = [(gain[at] * work[first + s, at] - shift[at]).astype(BF) for s in range(count)]
        spread = [
            (
                n,
                jnp.dot(
                    jnp.concatenate([g[s][a : a + n] for s in range(count)], axis=0),
                    cols_t[v],
                    preferred_element_type=F32,
                ).astype(BF),
            )
            for v, a, n in views_in(k)
        ]
        out = []
        for pair in range(0, count, 2):
            stack = jnp.concatenate(
                [
                    jnp.concatenate(
                        [
                            value[s * n : (s + 1) * n, p * cells : (p + 1) * cells]
                            for p in range(2)
                            for n, value in spread
                        ],
                        axis=0,
                    )
                    for s in (pair, pair + 1)
                ],
                axis=1,
            )
            both = jnp.dot(rows_t[k], stack, preferred_element_type=F32)
            out += [both[:, :cells], both[:, cells:]]
        return out

    def collect(k):
        def body(i, carry):
            for s, value in enumerate(terms(k, 4 * i, 4)):
                part[4 * i + s] = value if k == 0 else part[4 * i + s] + value
            return carry

        lax.fori_loop(0, slices // 4, body, 0)

    last = chunks - 1
    steps = []
    for k in range(chunks):
        steps += [(slab_of, k), (lead_of, k)]
        if k >= 1 and k < last:
            steps.append((share_of, k - 1))
    steps += [(share_of, last - 1)]
    for k in range(last):
        if k == 1 or last == 1:
            steps.append((share_of, last))
        steps += [(weigh, k), (collect, k)]
    steps.append((weigh, last))
    for do, k in steps:
        do(k)

    def merge(o):
        q = (y + o) % ny
        arrived(got.at[q], r4.at[q])
        summed[q] = keep[q] + got[q]
        if o:
            pending.append(send(summed.at[q], pieces.at[y], s5.at[q], r5.at[y], at_y(q)))

    order = y_off[::-1] + [0]
    for n, o in enumerate(order):
        q = (y + o) % ny
        for i in range(0, share, 2):
            first = (2 * q + 1 - core) * share + i
            for s, value in enumerate(terms(last, first, 2)):
                give[q, i + s] = part[first + s] + value
        pending.append(send(give.at[q], got.at[q], s4.at[q], r4.at[q], partner))
        for i in range(0, share, 2):
            first = (2 * q + core) * share + i
            for s, value in enumerate(terms(last, first, 2)):
                keep[q, i + s] = part[first + s] + value
        if n:
            merge(order[n - 1])
    merge(0)

    per = half // 8
    for v in range(2):
        for g in range(groups):
            image[pl.ds(2 * g + v, half, stride=2 * groups), :] = totals[
                g, v * per : (v + 1) * per
            ].reshape(half, 128)

    total = summed[y]
    for o in y_off:
        q = (y + o) % ny
        arrived(pieces.at[q], r5.at[q])
        total = total + pieces[q]
    grad[...] = total
    for copy in pending:
        copy.wait_send()
    for k in range(chunks):
        sent_totals(k)


def on_device(nx, nz, ny, density, row_index, row_weight, col_index, col_weight, assignment, target_image):
    slices, cells = density.shape[0], density.shape[1]
    views, flat = target_image.shape
    pixels = row_index.shape[1]
    wide, tiles = 2 * pixels, flat * views // (8 * 2 * pixels)
    chunks = tiles // nz
    share = slices // (2 * ny)
    lines = flat // 128
    vm = pl.BlockSpec(memory_space=pltpu.VMEM)
    dma = pltpu.SemaphoreType.DMA
    image, grad = pl.pallas_call(
        functools.partial(kernel, (nx, nz, ny, slices * nx * nz)),
        out_shape=(
            jax.ShapeDtypeStruct((views * lines, 128), F32),
            jax.ShapeDtypeStruct((share, cells, cells), F32),
        ),
        in_specs=[pl.BlockSpec(memory_space=pltpu.HBM)] * 7,
        out_specs=(vm, vm),
        scratch_shapes=[
            pltpu.SMEM(assignment.shape, jnp.int32),
            pltpu.VMEM(density.shape, BF),
            pltpu.VMEM(row_index.shape, jnp.int32),
            pltpu.VMEM(row_index.shape, F32),
            pltpu.VMEM(row_index.shape, jnp.int32),
            pltpu.VMEM(row_index.shape, F32),
            pltpu.VMEM((views * lines, 128), F32),
            dma((7,)),
            pltpu.VMEM((8, wide), jnp.int32),
            pltpu.VMEM((8, wide), F32),
            pltpu.VMEM((2, 2 * cells, cells), F32),
            pltpu.VMEM((wide, cells), BF),
            pltpu.VMEM((chunks, cells, 16 * nz), BF),
            pltpu.VMEM((2, 2 * cells, wide), BF),
            pltpu.VMEM((2, wide, 2 * cells), BF),
            pltpu.VMEM((slices, 8 * nz, 2 * cells), BF),
            pltpu.VMEM((slices, pixels, wide), F32),
            pltpu.VMEM((pixels, wide), F32),
            pltpu.VMEM((pixels, wide), F32),
            pltpu.VMEM((pixels, wide), F32),
            pltpu.VMEM((tiles, 2, 8, wide), F32),
            pltpu.VMEM((chunks, nz, 2, 8, wide), F32),
            pltpu.VMEM((chunks, nz, 2, 8, wide), F32),
            pltpu.VMEM((chunks, 2, 8, wide), F32),
            pltpu.VMEM((chunks, nx, 2, 8, wide), F32),
            pltpu.VMEM((chunks, nz, 2, 8, wide), F32),
            pltpu.VMEM((tiles, 2, 8, wide), F32),
            pltpu.VMEM((wide // 128, tiles, 8, 128), F32),
            pltpu.VMEM((slices, cells, cells), F32),
            pltpu.VMEM((ny, share, cells, cells), F32),
            pltpu.VMEM((ny, share, cells, cells), F32),
            pltpu.VMEM((ny, share, cells, cells), F32),
            pltpu.VMEM((ny, share, cells, cells), F32),
            pltpu.VMEM((ny, share, cells, cells), F32),
            dma((chunks, nz)), dma((chunks, nz)),
            dma((chunks, nx)), dma((chunks, nx)),
            dma((chunks, nz)), dma((chunks, nz)),
            dma((ny,)), dma((ny,)),
            dma((ny,)), dma((ny,)),
            dma((chunks, wide // 128, nz)), dma((chunks, wide // 128, nz)),
            dma((chunks, wide // 128, nx)), dma((chunks, wide // 128)),
        ],
        compiler_params=pltpu.CompilerParams(
            collective_id=0, has_side_effects=True, vmem_limit_bytes=67043328
        ),
    )(
        assignment, density, row_index, row_weight, col_index, col_weight,
        target_image.reshape(views, lines, 128).transpose(1, 0, 2).reshape(views * lines, 128),
    )
    return image.reshape(lines, views, 128).transpose(1, 0, 2).reshape(views, flat), grad


def solution(mesh, nz=ZDEV):
    placed = (P("depth", None, None), P(), P(), P(), P(), P("views"), P("views", None))
    nx, ny = mesh.shape["depth"] // nz, mesh.shape["views"] // 2
    return jax.shard_map(
        functools.partial(on_device, nx, nz, ny),
        mesh=mesh,
        in_specs=placed,
        out_specs=(P("views", None), P(("depth", "views"), None, None)),
        check_vma=False,
    )
```

time: 66.6 us -> 60.1 us (0.902)
  local copies, waits for them, and re-layouts: 6.89 us -> 2.39 us
  Pallas kernels: 58.6 us -> 56.9 us
    unnamed x16 -> x4, local copies, waits for them, and re-layouts: 6.89 us -> 2.39 us
    pallas_call x1, Pallas kernels: 58.6 us -> 56.9 us  [on_device(): pl.pallas_call(functools.partial(kernel, (nx, nz, ny, slices * nx * nz)),...]
where the time goes in v2:
time: 60.1 us; the launch traced here: 60 us
  Pallas kernels  56.9 us (95%)
  local copies, waits for them, and re-layouts  2.39 us (4%)
  between operations  0.65 us (1%)
    pallas_call x1, Pallas kernels, on_device(): pl.pallas_call(functools.partial(kernel, (nx, nz, ny, slices * nx * nz)),...  56.9 us
    unnamed x4, local copies, waits for them, and re-layouts  2.39 us

profile of v2, /device:TPU:1, one launch (start us, length us, event | category | flops | bytes accessed | tf_op | source)
XLA Modules:
  0.0 60.0 jit_solution(10271077081148281308)
XLA Ops:
  0.6 56.9 %shard_map.86 = (f32[576,128]{1,0:T(8,128)}, f32[2,128,128]{2,1,0:T(8,128)}) custom-call(s32[2]{0:T(128)} %refs_0_.1, bf16[16,128,128]{2,1,0:T(8,128)(2,1)} %refs_1_.1, s32[16,192]{1,0:T(8,128)} %refs_2_.1, f32[16,192]{1,0:T(8,128)} %refs_3_.1, s32[16,192]{1,0:T(8,128)} %refs_4_.1, f32[16,192]{1,0:T(8,128)} %refs_5_.1, f32[576,128]{1,0:T(8,128)} %bitcast.10), custom_call_target="tpu_custom_call" | custom-call | tf_op jit(solution)/shard_map/pallas_call | solution.py:400
  57.6 0.0 copy-start
  57.6 1.7 %copy.13 = f32[2,36864]{1,0:T(2,128)} copy(f32[2,36864]{1,0:T(2,128)} %bitcast.11) | data formatting | bytes 589824
  59.3 0.0 copy-done
  59.3 0.7 %copy.14 = f32[2,128,128]{2,1,0:T(8,128)} copy(f32[2,128,128]{2,1,0:T(8,128)S(1)} %copy-done) | data formatting | bytes 262144
Async XLA Ops:
  57.6 1.7 %copy-start = (f32[2,128,128]{2,1,0:T(8,128)S(1)}, f32[2,128,128]{2,1,0:T(8,128)}, u32[]{:S(2)}) copy-start(f32[2,128,128]{2,1,0:T(8,128)} %get-tuple-element.9) | copy-start | bytes 393220

commit v3 on v2

--- a/solution.py
+++ b/solution.py
@@ -30,7 +30,7 @@
     assign_h, density_h, row_index_h, row_weight_h, col_index_h, col_weight_h, target_h, image, grad,
     assign, density, row_index, row_weight, col_index, col_weight, target, loads,
     pad_i, pad_w, tall, rows_m, rows_t, cols_m, cols_t, crossed, work, goal, gain, shift,
-    mine, theirs, local, slab, slabs, back, final, totals, part, give, got, keep, summed, pieces,
+    mine, theirs, local, slab, slabs, back, final, totals, part, ended, got, summed, pieces,
     s1, r1, s2, r2, s3, r3, s4, r4, s5, r5, s6, r6, s7, r7,
     ) = refs
     nx, nz, ny, levels = dims
@@ -96,21 +96,25 @@
         zero = jnp.zeros((cells, lanes), F32)
         return jnp.where(places == idx, 1.0 - w, zero) + jnp.where(places == idx + 1, w, zero)
 
-    for v in range(2):
+    tall_rows = 8 * nz
+
+    def resamplers(v):
         tall[v] = resampler(v, 2 * cells).T
+        for p in range(2):
+            rows_m[p * pixels + v * half : p * pixels + (v + 1) * half, :] = tall[
+                v, pl.ds(p, half, stride=2), :
+            ].astype(BF)
         ct = resampler(2 + v, wide)
-        both = jnp.concatenate([ct, pltpu.roll(ct, pixels, 1)], axis=0)
-        cols_m[v] = both.astype(BF)
-        cols_t[v] = both.T.astype(BF)
-    rows = jnp.concatenate(
-        [tall[v, pl.ds(p, half, stride=2), :] for p in range(2) for v in range(2)], axis=0
-    )
-    rows_m[...] = rows.astype(BF)
-    tall_rows = 8 * nz
-    for k in range(chunks):
-        at = k * tall_rows
-        both = jnp.concatenate([rows[p * pixels + at : p * pixels + at + tall_rows] for p in range(2)], axis=0)
-        rows_t[k] = both.T.astype(BF)
+        cols_m[v] = jnp.concatenate([ct, pltpu.roll(ct, pixels, 1)], axis=0).astype(BF)
+
+    def transposed():
+        for v in range(2):
+            cols_t[v] = cols_m[v].T
+        for k in range(chunks):
+            at = k * tall_rows
+            rows_t[k] = jnp.concatenate(
+                [rows_m[p * pixels + at : p * pixels + at + tall_rows, :] for p in range(2)], axis=0
+            ).T
 
     def views_in(k):
         out = []
@@ -139,7 +143,7 @@
             )
             work[:, at + first : at + first + n, :] = out.reshape(slices, n, wide)
 
-    def march(tile, carry):
+    def march(tile):
         at = pl.ds(pl.multiple_of(tile * 8, 8), 8)
         through = jnp.ones((8, wide), F32)
         inclusive = jnp.zeros((8, wide), F32)
@@ -153,7 +157,6 @@
             through = through * att
         mine[tile, 0] = inclusive * (1.0 / step)
         mine[tile, 1] = through
-        return carry
 
     pending = []
 
@@ -170,14 +173,21 @@
         ).wait_recv()
 
     fetch[5].wait()
+    built = 0
     for k in range(chunks):
+        for v, _, _ in views_in(k):
+            if v >= built:
+                resamplers(v)
+                built = v + 1
         sample(k)
-        lax.fori_loop(k * nz, (k + 1) * nz, march, 0)
-        if k == 0:
-            pl.semaphore_wait(barrier, len(z_off) + len(x_off) + len(y_off) + 1)
         for o in z_off:
             q = (z + o) % nz
+            march(k * nz + q)
+            if k == 0 and o == z_off[0]:
+                pl.semaphore_wait(barrier, len(z_off) + len(x_off) + len(y_off) + 1)
             pending.append(send(mine.at[k * nz + q], theirs.at[k, z], s1.at[k, q], r1.at[k, z], at_z(q)))
+        march(k * nz + z)
+    transposed()
 
     fetch[6].wait()
     groups = wide // 128
@@ -348,22 +358,19 @@
     def merge(o):
         q = (y + o) % ny
         arrived(got.at[q], r4.at[q])
-        summed[q] = keep[q] + got[q]
+        summed[q] = ended[q, pl.ds(core * share, share)] + got[q]
         if o:
             pending.append(send(summed.at[q], pieces.at[y], s5.at[q], r5.at[y], at_y(q)))
 
     order = y_off[::-1] + [0]
     for n, o in enumerate(order):
         q = (y + o) % ny
-        for i in range(0, share, 2):
-            first = (2 * q + 1 - core) * share + i
-            for s, value in enumerate(terms(last, first, 2)):
-                give[q, i + s] = part[first + s] + value
-        pending.append(send(give.at[q], got.at[q], s4.at[q], r4.at[q], partner))
-        for i in range(0, share, 2):
-            first = (2 * q + core) * share + i
-            for s, value in enumerate(terms(last, first, 2)):
-                keep[q, i + s] = part[first + s] + value
+        first = 2 * q * share
+        for s, value in enumerate(terms(last, first, 2 * share)):
+            ended[q, s] = part[first + s] + value
+        pending.append(
+            send(ended.at[q, pl.ds((1 - core) * share, share)], got.at[q], s4.at[q], r4.at[q], partner)
+        )
         if n:
             merge(order[n - 1])
     merge(0)
@@ -435,8 +442,7 @@
             pltpu.VMEM((tiles, 2, 8, wide), F32),
             pltpu.VMEM((wide // 128, tiles, 8, 128), F32),
             pltpu.VMEM((slices, cells, cells), F32),
-            pltpu.VMEM((ny, share, cells, cells), F32),
-            pltpu.VMEM((ny, share, cells, cells), F32),
+            pltpu.VMEM((ny, 2 * share, cells, cells), F32),
             pltpu.VMEM((ny, share, cells, cells), F32),
             pltpu.VMEM((ny, share, cells, cells), F32),
             pltpu.VMEM((ny, share, cells, cells), F32),
@@ -449,12 +455,12 @@
             dma((chunks, wide // 128, nx)), dma((chunks, wide // 128)),
         ],
         compiler_params=pltpu.CompilerParams(
-            collective_id=0, has_side_effects=True, vmem_limit_bytes=67043328
+            collective_id=0, has_side_effects=True, vmem_limit_bytes=50331648
         ),
-    )(
+    )(*[pltpu.with_memory_space_constraint(a, pltpu.HBM) for a in (
         assignment, density, row_index, row_weight, col_index, col_weight,
         target_image.reshape(views, lines, 128).transpose(1, 0, 2).reshape(views * lines, 128),
-    )
+    )])
     return image.reshape(lines, views, 128).transpose(1, 0, 2).reshape(views, flat), grad
 
 

time: 60.1 us -> 57.7 us (0.960)
  Pallas kernels: 56.9 us -> 55.6 us
  local copies, waits for them, and re-layouts: 2.39 us -> 1.37 us
    pallas_call x1, Pallas kernels: 56.9 us -> 55.6 us  [on_device(): pl.pallas_call(functools.partial(kernel, (nx, nz, ny, slices * nx * nz)),...]
    unnamed x4 -> x2, local copies, waits for them, and re-layouts: 2.39 us -> 1.37 us
where the time goes in v3:
time: 57.7 us; the launch traced here: 57.6 us
  Pallas kernels  55.6 us (96%)
  local copies, waits for them, and re-layouts  1.37 us (2%)
  between operations  0.64 us (1%)
    pallas_call x1, Pallas kernels, on_device(): pl.pallas_call(functools.partial(kernel, (nx, nz, ny, slices * nx * nz)),...  55.6 us
    unnamed x2, local copies, waits for them, and re-layouts  1.37 us

profile of v3, /device:TPU:1, one launch (start us, length us, event | category | flops | bytes accessed | tf_op | source)
XLA Modules:
  0.0 57.6 jit_solution(13071542278075876827)
XLA Ops:
  0.6 55.6 %shard_map.86 = (f32[576,128]{1,0:T(8,128)S(1)}, f32[2,128,128]{2,1,0:T(8,128)S(1)}) custom-call(s32[2]{0:T(128)} %refs_0_.1, bf16[16,128,128]{2,1,0:T(8,128)(2,1)} %refs_1_.1, s32[16,192]{1,0:T(8,128)} %refs_2_.1, f32[16,192]{1,0:T(8,128)} %refs_3_.1, s32[16,192]{1,0:T(8,128)} %refs_4_.1, f32[16,192]{1,0:T(8,128)} %refs_5_.1, f32[576,128]{1,0:T(8,128)} %bitcast.11), custom_call_target="tpu_custom_call" | custom-call | tf_op jit(solution)/shard_map/pallas_call | solution.py:407
  56.3 0.7 %copy.13 = f32[2,36864]{1,0:T(2,128)} copy(f32[2,36864]{1,0:T(2,128)S(1)} %bitcast.10) | data formatting | bytes 589824
  57.0 0.7 %copy.14 = f32[2,128,128]{2,1,0:T(8,128)} copy(f32[2,128,128]{2,1,0:T(8,128)S(1)} %get-tuple-element.9) | data formatting | bytes 262144

commit v4 on v3

--- a/solution.py
+++ b/solution.py
@@ -30,8 +30,9 @@
     assign_h, density_h, row_index_h, row_weight_h, col_index_h, col_weight_h, target_h, image, grad,
     assign, density, row_index, row_weight, col_index, col_weight, target, loads,
     pad_i, pad_w, tall, rows_m, rows_t, cols_m, cols_t, crossed, work, goal, gain, shift,
-    mine, theirs, local, slab, slabs, back, final, totals, part, ended, got, summed, pieces,
-    s1, r1, s2, r2, s3, r3, s4, r4, s5, r5, s6, r6, s7, r7,
+    mine, theirs, local, slab, slabs, back, final, totals, part, ended, got, summed, pieces, relay, passed,
+    mass, masses, slab_mass, slab_masses, before, ahead,
+    s1, r1, s2, r2, s3, r3, s4, r4, s5, r5, s6, r6, s7, r7, s8, r8, s9, r9, s10, r10, s11, r11,
     ) = refs
     nx, nz, ny, levels = dims
     step = 1.5 / levels
@@ -41,6 +42,9 @@
     wide = 2 * pixels
     chunks = 2 * half // 8 // nz
     share = slices // (2 * ny)
+    groups = wide // 128
+    last = chunks - 1
+    units = [(k, slice(0, groups)) for k in range(last)] + [(last, slice(g, g + 1)) for g in range(groups)]
     depth, vw = lax.axis_index("depth"), lax.axis_index("views")
     x, z = depth // nz, depth % nz
     y, core = vw // 2, vw % 2
@@ -55,6 +59,8 @@
         return (depth, q * 2 + core)
 
     partner = (depth, y * 2 + 1 - core)
+    beside = spread_order(2 * ny)
+    rows_held = cells // (2 * ny)
     z_off, x_off, y_off = spread_order(nz), spread_order(nx), spread_order(ny)
 
     fetch = [
@@ -75,9 +81,8 @@
         pl.semaphore_signal(barrier, inc=1, device_id=at_z((z + o) % nz), device_id_type=MESH)
     for o in x_off:
         pl.semaphore_signal(barrier, inc=1, device_id=at_x((x + o) % nx), device_id_type=MESH)
-    for o in y_off:
-        pl.semaphore_signal(barrier, inc=1, device_id=at_y((y + o) % ny), device_id_type=MESH)
-    pl.semaphore_signal(barrier, inc=1, device_id=partner, device_id_type=MESH)
+    for o in beside:
+        pl.semaphore_signal(barrier, inc=1, device_id=(depth, (vw + o) % (2 * ny)), device_id_type=MESH)
 
     for copy in fetch[:5]:
         copy.wait()
@@ -155,8 +160,10 @@
             inclusive = inclusive + through * (optical * gone)
             work[s, at, :] = through * (gone + optical * att) + inclusive
             through = through * att
-        mine[tile, 0] = inclusive * (1.0 / step)
-        mine[tile, 1] = through
+        for g in range(groups):
+            lanes = slice(g * 128, (g + 1) * 128)
+            mine[tile, g, 0] = inclusive[:, lanes] * (1.0 / step)
+            mine[tile, g, 1] = through[:, lanes]
 
     pending = []
 
@@ -172,81 +179,152 @@
             src_ref=dst, dst_ref=dst, send_sem=rsem, recv_sem=rsem, device_id=partner, device_id_type=MESH
         ).wait_recv()
 
-    fetch[5].wait()
+    def mass_sent():
+        held = density[:, pl.ds(pl.multiple_of(vw * rows_held, rows_held), rows_held), :]
+        one = jnp.sum(held.astype(F32), axis=0)
+        mass[...] = one
+        masses[z] = one
+        for o in z_off:
+            q = (z + o) % nz
+            pending.append(send(mass, masses.at[z], s8.at[q], r8.at[z], at_z(q)))
+
+    def mass_along_z():
+        for o in z_off:
+            q = (z + o) % nz
+            arrived(masses.at[q], r8.at[q])
+        lead = jnp.zeros((rows_held, cells), F32)
+        total = lead
+        for q in range(nz):
+            lead = jnp.where(q == z, total, lead)
+            total = total + masses[q]
+        slab_mass[...] = total
+        before[vw] = lead
+        for o in x_off:
+            q = (x + o) % nx
+            pending.append(send(slab_mass, slab_masses.at[x], s9.at[q], r9.at[x], at_x(q)))
+
+    def mass_along_x():
+        slab_masses[x] = jnp.zeros((rows_held, cells), F32)
+        for o in x_off:
+            q = (x + o) % nx
+            arrived(slab_masses.at[q], r9.at[q])
+        lead = before[vw]
+        for q in range(nx):
+            lead = lead + jnp.where(q < x, slab_masses[q], 0.0)
+        before[vw] = lead
+        for o in beside:
+            q = (vw + o) % (2 * ny)
+            pending.append(send(before.at[vw], before.at[vw], s10.at[q], r10.at[vw], (depth, q)))
+
+    def split(value):
+        high = value.astype(BF)
+        return high, (value - high.astype(F32)).astype(BF)
+
+    def see_ahead():
+        for o in beside:
+            q = (vw + o) % (2 * ny)
+            arrived(before.at[q], r10.at[q])
+        two = jnp.concatenate(split(before[...].reshape(cells, cells)), axis=1)
+        out = jnp.dot(rows_m[...], two, preferred_element_type=F32)
+        out = out[:, :cells] + out[:, cells:]
+        parts = split(jnp.concatenate([out[:pixels], out[pixels:]], axis=1))
+        for v in range(2):
+            at = slice(v * half, (v + 1) * half)
+            passed = sum(jnp.dot(part[at], cols_m[v], preferred_element_type=F32) for part in parts)
+            ahead[at] = jnp.exp2(passed * (-step * LOG2E))
+
+    def send_share(u, q):
+        k, gs = units[u]
+        pending.append(
+            send(mine.at[k * nz + q, gs], theirs.at[k, z, gs], s1.at[u, q], r1.at[u, z], at_z(q))
+        )
+
     built = 0
     for k in range(chunks):
         for v, _, _ in views_in(k):
             if v >= built:
                 resamplers(v)
                 built = v + 1
+        if k == 0:
+            fetch[5].wait()
         sample(k)
-        for o in z_off:
-            q = (z + o) % nz
+        for q in range(nz):
             march(k * nz + q)
-            if k == 0 and o == z_off[0]:
-                pl.semaphore_wait(barrier, len(z_off) + len(x_off) + len(y_off) + 1)
-            pending.append(send(mine.at[k * nz + q], theirs.at[k, z], s1.at[k, q], r1.at[k, z], at_z(q)))
-        march(k * nz + z)
+        if k == 0:
+            pl.semaphore_wait(barrier, len(z_off) + len(x_off) + len(beside))
+        for u in [k] if k < last else range(last, len(units)):
+            for o in z_off:
+                send_share(u, (z + o) % nz)
+        if k == 0:
+            mass_sent()
     transposed()
 
     fetch[6].wait()
-    groups = wide // 128
     for v in range(2):
         for g in range(groups):
             goal[v * half : (v + 1) * half, g * 128 : (g + 1) * 128] = target[
                 pl.ds(2 * g + v, half, stride=2 * groups), :
             ]
 
-    def slab_of(k):
-        theirs[k, z] = mine[k * nz + z]
+    def slab_of(u):
+        k, gs = units[u]
+        theirs[k, z, gs] = mine[k * nz + z, gs]
         for o in z_off:
             q = (z + o) % nz
-            arrived(theirs.at[k, q], r1.at[k, q])
-        c = jnp.zeros((8, wide), F32)
-        t = jnp.ones((8, wide), F32)
+            arrived(theirs.at[k, q, gs], r1.at[u, q])
+        c = jnp.zeros((gs.stop - gs.start, 8, 128), F32)
+        t = jnp.ones((gs.stop - gs.start, 8, 128), F32)
         for q in range(nz):
-            local[k, q, 0] = c
-            local[k, q, 1] = t
-            c = c + t * theirs[k, q, 0]
-            t = t * theirs[k, q, 1]
-        slab[k, 0] = c
-        slab[k, 1] = t
-        slabs[k, x, 0] = c
-        slabs[k, x, 1] = t
+            local[k, q, gs] = c
+            c = c + t * theirs[k, q, gs, 0]
+            t = t * theirs[k, q, gs, 1]
+        slab[k, gs, 0] = c
+        slab[k, gs, 1] = t
+        slabs[k, x, gs, 0] = c
+        slabs[k, x, gs, 1] = t
         for o in x_off:
             q = (x + o) % nx
-            pending.append(send(slab.at[k], slabs.at[k, x], s2.at[k, q], r2.at[k, x], at_x(q)))
-
-    def lead_of(k):
+            pending.append(send(slab.at[k, gs], slabs.at[k, x, gs], s2.at[u, q], r2.at[u, x], at_x(q)))
+
+    def lead_of(u):
+        k, gs = units[u]
         for o in x_off:
             q = (x + o) % nx
-            arrived(slabs.at[k, q], r2.at[k, q])
-        lead_c = jnp.zeros((8, wide), F32)
-        lead_t = jnp.ones((8, wide), F32)
+            arrived(slabs.at[k, q, gs], r2.at[u, q])
+        lead_c = jnp.zeros((gs.stop - gs.start, 8, 128), F32)
+        lead_t = jnp.ones((gs.stop - gs.start, 8, 128), F32)
         c, t = lead_c, lead_t
         for q in range(nx):
-            c = c + t * slabs[k, q, 0]
-            t = t * slabs[k, q, 1]
+            c = c + t * slabs[k, q, gs, 0]
+            t = t * slabs[k, q, gs, 1]
             earlier = q < x
             lead_c = jnp.where(earlier, c, lead_c)
             lead_t = jnp.where(earlier, t, lead_t)
         own = k * nz + z
-        for g in range(groups):
-
-            @pl.when(x == g % nx)
-            def _():
-                totals[g, own] = c[:, g * 128 : (g + 1) * 128]
-                for o in z_off:
-                    q = (z + o) % nz
+        if k == last:
+            g = gs.start
+            totals[g, own] = c[0]
+            for o in z_off:
+                q = (z + o) % nz
+                pending.append(
                     send(totals.at[g, own], totals.at[g, own], s6.at[k, g, q], r6.at[k, g, z], at_z(q))
+                )
+        else:
+            for g in range(groups):
+
+                @pl.when(x == g % nx)
+                def _():
+                    totals[g, own] = c[g]
+                    for o in z_off:
+                        q = (z + o) % nz
+                        send(totals.at[g, own], totals.at[g, own], s6.at[k, g, q], r6.at[k, g, z], at_z(q))
 
         for q in range(nz):
-            back[k, q, 0] = lead_t * local[k, q, 1]
-            back[k, q, 1] = c - (lead_c + lead_t * local[k, q, 0])
+            back[k, q, gs] = c - (lead_c + lead_t * local[k, q, gs])
         for o in z_off:
             q = (z + o) % nz
-            pending.append(send(back.at[k, q], final.at[own], s3.at[k, q], r3.at[k, z], at_z(q)))
-        final[own] = back[k, z]
+            pending.append(send(back.at[k, q, gs], final.at[own, gs], s3.at[u, q], r3.at[u, z], at_z(q)))
+        final[own, gs] = back[k, z, gs]
 
     def share_of(k):
         for g in range(groups):
@@ -282,21 +360,29 @@
                     ).wait_send()
 
     def weigh(k):
-        for o in z_off:
-            q = (z + o) % nz
-            arrived(final.at[k * nz + q], r3.at[k, q])
+        for u, (j, gs) in enumerate(units):
+            if j == k:
+                for o in z_off:
+                    q = (z + o) % nz
+                    arrived(final.at[k * nz + q, gs], r3.at[u, q])
         for g in range(groups):
-
-            @pl.when(x != g % nx)
-            def _():
-                arrived(totals.at[g, k * nz : (k + 1) * nz], r7.at[k, g])
+            if k == last:
+                for o in z_off:
+                    q = (z + o) % nz
+                    arrived(totals.at[g, k * nz + q], r6.at[k, g, q])
+            else:
+
+                @pl.when(x != g % nx)
+                def _():
+                    arrived(totals.at[g, k * nz : (k + 1) * nz], r7.at[k, g])
 
         at = slice(k * tall_rows, (k + 1) * tall_rows)
         tiles = slice(k * nz, (k + 1) * nz)
         total = jnp.concatenate([totals[g, tiles].reshape(tall_rows, 128) for g in range(groups)], axis=1)
         residue = levels * (total - goal[at])
-        gain[at] = residue * final[tiles, 0].reshape(tall_rows, wide)
-        shift[at] = step * residue * final[tiles, 1].reshape(tall_rows, wide)
+        gain[at] = residue * ahead[at]
+        behind = jnp.concatenate([final[tiles, g].reshape(tall_rows, 128) for g in range(groups)], axis=1)
+        shift[at] = step * residue * behind
 
     def terms(k, first, count):
         at = slice(k * tall_rows, (k + 1) * tall_rows)
@@ -340,27 +426,50 @@
 
         lax.fori_loop(0, slices // 4, body, 0)
 
-    last = chunks - 1
-    steps = []
-    for k in range(chunks):
-        steps += [(slab_of, k), (lead_of, k)]
-        if k >= 1 and k < last:
-            steps.append((share_of, k - 1))
-    steps += [(share_of, last - 1)]
+    slab_of(0)
+    mass_along_z()
+    lead_of(0)
+    mass_along_x()
+    for k in range(1, last):
+        slab_of(k)
+        if k == last - 1:
+            slab_of(last)
+        lead_of(k)
+        share_of(k - 1)
+    see_ahead()
+    for u in range(last + 1, len(units)):
+        slab_of(u)
+    for u in range(last, len(units)):
+        lead_of(u)
+    share_of(last - 1)
     for k in range(last):
-        if k == 1 or last == 1:
-            steps.append((share_of, last))
-        steps += [(weigh, k), (collect, k)]
-    steps.append((weigh, last))
-    for do, k in steps:
-        do(k)
+        weigh(k)
+        collect(k)
+    weigh(last)
+
+    up, down = (y + 1) % ny, (y + ny - 1) % ny
+    halves = slice(0, share // 2), slice(share // 2, share)
+
+    def give_half(n, src, q):
+        pending.append(send(src, pieces.at[y, halves[n]], s5.at[q, n], r5.at[y, n], at_y(q)))
 
     def merge(o):
         q = (y + o) % ny
         arrived(got.at[q], r4.at[q])
         summed[q] = ended[q, pl.ds(core * share, share)] + got[q]
-        if o:
-            pending.append(send(summed.at[q], pieces.at[y], s5.at[q], r5.at[y], at_y(q)))
+        if o == 2:
+            for n, near in enumerate((up, down)):
+                pending.append(send(summed.at[q, halves[n]], relay.at[n], s11.at[n], r11.at[n], at_y(near)))
+        elif o == 1:
+            give_half(1, summed.at[q, halves[1]], q)
+        elif o == 3:
+            give_half(0, summed.at[q, halves[0]], q)
+
+    def pass_on():
+        for n, near in enumerate((up, down)):
+            arrived(relay.at[n], r11.at[n])
+            passed[n] = summed[near, halves[n]] + relay[n]
+            give_half(n, passed.at[n], near)
 
     order = y_off[::-1] + [0]
     for n, o in enumerate(order):
@@ -374,6 +483,7 @@
         if n:
             merge(order[n - 1])
     merge(0)
+    pass_on()
 
     per = half // 8
     for v in range(2):
@@ -383,14 +493,14 @@
             ].reshape(half, 128)
 
     total = summed[y]
-    for o in y_off:
-        q = (y + o) % ny
-        arrived(pieces.at[q], r5.at[q])
+    for q in (down, up):
+        for n in range(2):
+            arrived(pieces.at[q, halves[n]], r5.at[q, n])
         total = total + pieces[q]
     grad[...] = total
     for copy in pending:
         copy.wait_send()
-    for k in range(chunks):
+    for k in range(last):
         sent_totals(k)
 
 
@@ -402,6 +512,8 @@
     chunks = tiles // nz
     share = slices // (2 * ny)
     lines = flat // 128
+    groups = wide // 128
+    units = chunks - 1 + groups
     vm = pl.BlockSpec(memory_space=pltpu.VMEM)
     dma = pltpu.SemaphoreType.DMA
     image, grad = pl.pallas_call(
@@ -433,26 +545,38 @@
             pltpu.VMEM((pixels, wide), F32),
             pltpu.VMEM((pixels, wide), F32),
             pltpu.VMEM((pixels, wide), F32),
-            pltpu.VMEM((tiles, 2, 8, wide), F32),
-            pltpu.VMEM((chunks, nz, 2, 8, wide), F32),
-            pltpu.VMEM((chunks, nz, 2, 8, wide), F32),
-            pltpu.VMEM((chunks, 2, 8, wide), F32),
-            pltpu.VMEM((chunks, nx, 2, 8, wide), F32),
-            pltpu.VMEM((chunks, nz, 2, 8, wide), F32),
-            pltpu.VMEM((tiles, 2, 8, wide), F32),
-            pltpu.VMEM((wide // 128, tiles, 8, 128), F32),
+            pltpu.VMEM((tiles, groups, 2, 8, 128), F32),
+            pltpu.VMEM((chunks, nz, groups, 2, 8, 128), F32),
+            pltpu.VMEM((chunks, nz, groups, 8, 128), F32),
+            pltpu.VMEM((chunks, groups, 2, 8, 128), F32),
+            pltpu.VMEM((chunks, nx, groups, 2, 8, 128), F32),
+            pltpu.VMEM((chunks, nz, groups, 8, 128), F32),
+            pltpu.VMEM((tiles, groups, 8, 128), F32),
+            pltpu.VMEM((groups, tiles, 8, 128), F32),
             pltpu.VMEM((slices, cells, cells), F32),
             pltpu.VMEM((ny, 2 * share, cells, cells), F32),
             pltpu.VMEM((ny, share, cells, cells), F32),
             pltpu.VMEM((ny, share, cells, cells), F32),
             pltpu.VMEM((ny, share, cells, cells), F32),
-            dma((chunks, nz)), dma((chunks, nz)),
-            dma((chunks, nx)), dma((chunks, nx)),
-            dma((chunks, nz)), dma((chunks, nz)),
+            pltpu.VMEM((2, share // 2, cells, cells), F32),
+            pltpu.VMEM((2, share // 2, cells, cells), F32),
+            pltpu.VMEM((cells // (2 * ny), cells), F32),
+            pltpu.VMEM((nz, cells // (2 * ny), cells), F32),
+            pltpu.VMEM((cells // (2 * ny), cells), F32),
+            pltpu.VMEM((nx, cells // (2 * ny), cells), F32),
+            pltpu.VMEM((2 * ny, cells // (2 * ny), cells), F32),
+            pltpu.VMEM((pixels, wide), F32),
+            dma((units, nz)), dma((units, nz)),
+            dma((units, nx)), dma((units, nx)),
+            dma((units, nz)), dma((units, nz)),
             dma((ny,)), dma((ny,)),
-            dma((ny,)), dma((ny,)),
-            dma((chunks, wide // 128, nz)), dma((chunks, wide // 128, nz)),
-            dma((chunks, wide // 128, nx)), dma((chunks, wide // 128)),
+            dma((ny, 2)), dma((ny, 2)),
+            dma((chunks, groups, nz)), dma((chunks, groups, nz)),
+            dma((chunks, groups, nx)), dma((chunks, groups)),
+            dma((nz,)), dma((nz,)),
+            dma((nx,)), dma((nx,)),
+            dma((2 * ny,)), dma((2 * ny,)),
+            dma((2,)), dma((2,)),
         ],
         compiler_params=pltpu.CompilerParams(
             collective_id=0, has_side_effects=True, vmem_limit_bytes=50331648

time: 57.7 us -> 55.1 us (0.955)
  Pallas kernels: 55.6 us -> 53 us
    pallas_call x1, Pallas kernels: 55.6 us -> 53 us  [on_device(): pl.pallas_call(functools.partial(kernel, (nx, nz, ny, slices * nx * nz)),...]
where the time goes in v4:
time: 55.1 us; the launch traced here: 55 us
  Pallas kernels  53 us (96%)
  local copies, waits for them, and re-layouts  1.37 us (2%)
  between operations  0.64 us (1%)
    pallas_call x1, Pallas kernels, on_device(): pl.pallas_call(functools.partial(kernel, (nx, nz, ny, slices * nx * nz)),...  53 us
    unnamed x2, local copies, waits for them, and re-layouts  1.37 us

profile of v4, /device:TPU:1, one launch (start us, length us, event | category | flops | bytes accessed | tf_op | source)
XLA Modules:
  0.0 55.0 jit_solution(5730798140638281116)
XLA Ops:
  0.6 53.0 %shard_map.86 = (f32[576,128]{1,0:T(8,128)S(1)}, f32[2,128,128]{2,1,0:T(8,128)S(1)}) custom-call(s32[2]{0:T(128)} %refs_0_.1, bf16[16,128,128]{2,1,0:T(8,128)(2,1)} %refs_1_.1, s32[16,192]{1,0:T(8,128)} %refs_2_.1, f32[16,192]{1,0:T(8,128)} %refs_3_.1, s32[16,192]{1,0:T(8,128)} %refs_4_.1, f32[16,192]{1,0:T(8,128)} %refs_5_.1, f32[576,128]{1,0:T(8,128)} %bitcast.11), custom_call_target="tpu_custom_call" | custom-call | tf_op jit(solution)/shard_map/pallas_call | solution.py:519
  53.6 0.7 %copy.13 = f32[2,36864]{1,0:T(2,128)} copy(f32[2,36864]{1,0:T(2,128)S(1)} %bitcast.10) | data formatting | bytes 589824
  54.3 0.7 %copy.14 = f32[2,128,128]{2,1,0:T(8,128)} copy(f32[2,128,128]{2,1,0:T(8,128)S(1)} %get-tuple-element.9) | data formatting | bytes 262144

commit v5 on v4

--- a/solution.py
+++ b/solution.py
@@ -44,7 +44,7 @@
     share = slices // (2 * ny)
     groups = wide // 128
     last = chunks - 1
-    units = [(k, slice(0, groups)) for k in range(last)] + [(last, slice(g, g + 1)) for g in range(groups)]
+    units = [(k, slice(0, groups)) for k in range(last)] + [(last, slice(0, 2)), (last, slice(2, groups))]
     depth, vw = lax.axis_index("depth"), lax.axis_index("views")
     x, z = depth // nz, depth % nz
     y, core = vw // 2, vw % 2
@@ -61,7 +61,7 @@
     partner = (depth, y * 2 + 1 - core)
     beside = spread_order(2 * ny)
     rows_held = cells // (2 * ny)
-    z_off, x_off, y_off = spread_order(nz), spread_order(nx), spread_order(ny)
+    z_off, x_off, y_off = (spread_order(n)[::-1] for n in (nz, nx, ny))
 
     fetch = [
         pltpu.make_async_copy(src, dst, loads.at[n])
@@ -302,13 +302,13 @@
             lead_t = jnp.where(earlier, t, lead_t)
         own = k * nz + z
         if k == last:
-            g = gs.start
-            totals[g, own] = c[0]
+            for g in range(gs.start, gs.stop):
+                totals[g, own] = c[g - gs.start]
             for o in z_off:
                 q = (z + o) % nz
-                pending.append(
-                    send(totals.at[g, own], totals.at[g, own], s6.at[k, g, q], r6.at[k, g, z], at_z(q))
-                )
+                for g in range(gs.start, gs.stop):
+                    one = totals.at[g, own]
+                    pending.append(send(one, one, s6.at[k, g, q], r6.at[k, g, z], at_z(q)))
         else:
             for g in range(groups):
 
@@ -471,7 +471,7 @@
             passed[n] = summed[near, halves[n]] + relay[n]
             give_half(n, passed.at[n], near)
 
-    order = y_off[::-1] + [0]
+    order = y_off + [0]
     for n, o in enumerate(order):
         q = (y + o) % ny
         first = 2 * q * share
@@ -502,6 +502,17 @@
         copy.wait_send()
     for k in range(last):
         sent_totals(k)
+
+
+def write_out(image, grad, image_out, grad_out, sems):
+    copies = [
+        pltpu.make_async_copy(src, dst, sems.at[n])
+        for n, (src, dst) in enumerate(((image, image_out), (grad, grad_out)))
+    ]
+    for copy in copies:
+        copy.start()
+    for copy in copies:
+        copy.wait()
 
 
 def on_device(nx, nz, ny, density, row_index, row_weight, col_index, col_weight, assignment, target_image):
@@ -585,6 +596,17 @@
         assignment, density, row_index, row_weight, col_index, col_weight,
         target_image.reshape(views, lines, 128).transpose(1, 0, 2).reshape(views * lines, 128),
     )])
+    image, grad = pl.pallas_call(
+        write_out,
+        out_shape=(
+            jax.ShapeDtypeStruct(image.shape, F32),
+            jax.ShapeDtypeStruct(grad.shape, F32),
+        ),
+        in_specs=[vm, vm],
+        out_specs=(pl.BlockSpec(memory_space=pltpu.HBM),) * 2,
+        scratch_shapes=[dma((2,))],
+        compiler_params=pltpu.CompilerParams(vmem_limit_bytes=1 << 20),
+    )(image, grad)
     return image.reshape(lines, views, 128).transpose(1, 0, 2).reshape(views, flat), grad
 
 

time: 55.1 us -> 53.4 us (0.969)
  local copies, waits for them, and re-layouts: 1.37 us -> 0 us
    unnamed x2 -> x0, local copies, waits for them, and re-layouts: 1.37 us -> none
    pallas_call x1, Pallas kernels: 53 us -> 51.9 us  [on_device(): pl.pallas_call(functools.partial(kernel, (nx, nz, ny, slices * nx * nz)),...]
    pallas_call x0 -> x1, Pallas kernels: none -> 0.77 us  [on_device(): pl.pallas_call(write_out, out_shape=(jax.ShapeDtypeStruct(image.shape, F3...]
where the time goes in v5:
time: 53.4 us; the launch traced here: 53.3 us
  Pallas kernels  52.7 us (99%)
  between operations  0.64 us (1%)
    pallas_call x1, Pallas kernels, on_device(): pl.pallas_call(functools.partial(kernel, (nx, nz, ny, slices * nx * nz)),...  51.9 us

profile of v5, /device:TPU:1, one launch (start us, length us, event | category | flops | bytes accessed | tf_op | source)
XLA Modules:
  0.0 53.3 jit_solution(8826546155219627626)
XLA Ops:
  0.6 51.9 %shard_map.86 = (f32[576,128]{1,0:T(8,128)S(1)}, f32[2,128,128]{2,1,0:T(8,128)S(1)}) custom-call(s32[2]{0:T(128)} %refs_0_.1, bf16[16,128,128]{2,1,0:T(8,128)(2,1)} %refs_1_.1, s32[16,192]{1,0:T(8,128)} %refs_2_.1, f32[16,192]{1,0:T(8,128)} %refs_3_.1, s32[16,192]{1,0:T(8,128)} %refs_4_.1, f32[16,192]{1,0:T(8,128)} %refs_5_.1, f32[576,128]{1,0:T(8,128)} %bitcast.10), custom_call_target="tpu_custom_call" | custom-call | tf_op jit(solution)/shard_map/pallas_call | solution.py:530
  52.5 0.8 %shard_map.87 = (f32[576,128]{1,0:T(8,128)}, f32[2,128,128]{2,1,0:T(8,128)}) custom-call(f32[576,128]{1,0:T(8,128)S(1)} %get-tuple-element.6.image, f32[2,128,128]{2,1,0:T(8,128)S(1)} %get-tuple-element.7.grad), custom_call_target="tpu_custom_call" | custom-call | tf_op jit(solution)/shard_map/pallas_call | solution.py:599

commit v6 on v5

--- a/solution.py
+++ b/solution.py
@@ -30,9 +30,9 @@
     assign_h, density_h, row_index_h, row_weight_h, col_index_h, col_weight_h, target_h, image, grad,
     assign, density, row_index, row_weight, col_index, col_weight, target, loads,
     pad_i, pad_w, tall, rows_m, rows_t, cols_m, cols_t, crossed, work, goal, gain, shift,
-    mine, theirs, local, slab, slabs, back, final, totals, part, ended, got, summed, pieces, relay, passed,
+    mine, theirs, local, slab, slabs, back, final, part, ended, got, summed, pieces, relay, passed,
     mass, masses, slab_mass, slab_masses, before, ahead,
-    s1, r1, s2, r2, s3, r3, s4, r4, s5, r5, s6, r6, s7, r7, s8, r8, s9, r9, s10, r10, s11, r11,
+    s1, r1, s2, r2, s3, r3, s4, r4, s5, r5, s8, r8, s9, r9, s10, r10, s11, r11,
     ) = refs
     nx, nz, ny, levels = dims
     step = 1.5 / levels
@@ -301,63 +301,13 @@
             lead_c = jnp.where(earlier, c, lead_c)
             lead_t = jnp.where(earlier, t, lead_t)
         own = k * nz + z
-        if k == last:
-            for g in range(gs.start, gs.stop):
-                totals[g, own] = c[g - gs.start]
-            for o in z_off:
-                q = (z + o) % nz
-                for g in range(gs.start, gs.stop):
-                    one = totals.at[g, own]
-                    pending.append(send(one, one, s6.at[k, g, q], r6.at[k, g, z], at_z(q)))
-        else:
-            for g in range(groups):
-
-                @pl.when(x == g % nx)
-                def _():
-                    totals[g, own] = c[g]
-                    for o in z_off:
-                        q = (z + o) % nz
-                        send(totals.at[g, own], totals.at[g, own], s6.at[k, g, q], r6.at[k, g, z], at_z(q))
-
         for q in range(nz):
-            back[k, q, gs] = c - (lead_c + lead_t * local[k, q, gs])
+            back[k, q, gs, 0] = c - (lead_c + lead_t * local[k, q, gs])
+            back[k, q, gs, 1] = c
         for o in z_off:
             q = (z + o) % nz
             pending.append(send(back.at[k, q, gs], final.at[own, gs], s3.at[u, q], r3.at[u, z], at_z(q)))
         final[own, gs] = back[k, z, gs]
-
-    def share_of(k):
-        for g in range(groups):
-
-            @pl.when(x == g % nx)
-            def _():
-                for o in z_off:
-                    q = (z + o) % nz
-                    arrived(totals.at[g, k * nz + q], r6.at[k, g, q])
-                for o in x_off:
-                    q = (x + o) % nx
-                    tiles = totals.at[g, k * nz : (k + 1) * nz]
-                    send(tiles, tiles, s7.at[k, g, q], r7.at[k, g], at_x(q))
-
-    def sent_totals(k):
-        for g in range(groups):
-
-            @pl.when(x == g % nx)
-            def _():
-                one = totals.at[g, k * nz + z]
-                tiles = totals.at[g, k * nz : (k + 1) * nz]
-                for o in z_off:
-                    q = (z + o) % nz
-                    pltpu.make_async_remote_copy(
-                        src_ref=one, dst_ref=one, send_sem=s6.at[k, g, q], recv_sem=r6.at[k, g, z],
-                        device_id=at_z(q), device_id_type=MESH,
-                    ).wait_send()
-                for o in x_off:
-                    q = (x + o) % nx
-                    pltpu.make_async_remote_copy(
-                        src_ref=tiles, dst_ref=tiles, send_sem=s7.at[k, g, q], recv_sem=r7.at[k, g],
-                        device_id=at_x(q), device_id_type=MESH,
-                    ).wait_send()
 
     def weigh(k):
         for u, (j, gs) in enumerate(units):
@@ -365,23 +315,12 @@
                 for o in z_off:
                     q = (z + o) % nz
                     arrived(final.at[k * nz + q, gs], r3.at[u, q])
-        for g in range(groups):
-            if k == last:
-                for o in z_off:
-                    q = (z + o) % nz
-                    arrived(totals.at[g, k * nz + q], r6.at[k, g, q])
-            else:
-
-                @pl.when(x != g % nx)
-                def _():
-                    arrived(totals.at[g, k * nz : (k + 1) * nz], r7.at[k, g])
-
         at = slice(k * tall_rows, (k + 1) * tall_rows)
         tiles = slice(k * nz, (k + 1) * nz)
-        total = jnp.concatenate([totals[g, tiles].reshape(tall_rows, 128) for g in range(groups)], axis=1)
+        total = jnp.concatenate([final[tiles, g, 1].reshape(tall_rows, 128) for g in range(groups)], axis=1)
         residue = levels * (total - goal[at])
         gain[at] = residue * ahead[at]
-        behind = jnp.concatenate([final[tiles, g].reshape(tall_rows, 128) for g in range(groups)], axis=1)
+        behind = jnp.concatenate([final[tiles, g, 0].reshape(tall_rows, 128) for g in range(groups)], axis=1)
         shift[at] = step * residue * behind
 
     def terms(k, first, count):
@@ -435,13 +374,11 @@
         if k == last - 1:
             slab_of(last)
         lead_of(k)
-        share_of(k - 1)
     see_ahead()
     for u in range(last + 1, len(units)):
         slab_of(u)
     for u in range(last, len(units)):
         lead_of(u)
-    share_of(last - 1)
     for k in range(last):
         weigh(k)
         collect(k)
@@ -488,8 +425,8 @@
     per = half // 8
     for v in range(2):
         for g in range(groups):
-            image[pl.ds(2 * g + v, half, stride=2 * groups), :] = totals[
-                g, v * per : (v + 1) * per
+            image[pl.ds(2 * g + v, half, stride=2 * groups), :] = final[
+                v * per : (v + 1) * per, g, 1
             ].reshape(half, 128)
 
     total = summed[y]
@@ -500,8 +437,6 @@
     grad[...] = total
     for copy in pending:
         copy.wait_send()
-    for k in range(last):
-        sent_totals(k)
 
 
 def write_out(image, grad, image_out, grad_out, sems):
@@ -561,9 +496,8 @@
             pltpu.VMEM((chunks, nz, groups, 8, 128), F32),
             pltpu.VMEM((chunks, groups, 2, 8, 128), F32),
             pltpu.VMEM((chunks, nx, groups, 2, 8, 128), F32),
-            pltpu.VMEM((chunks, nz, groups, 8, 128), F32),
-            pltpu.VMEM((tiles, groups, 8, 128), F32),
-            pltpu.VMEM((groups, tiles, 8, 128), F32),
+            pltpu.VMEM((chunks, nz, groups, 2, 8, 128), F32),
+            pltpu.VMEM((tiles, groups, 2, 8, 128), F32),
             pltpu.VMEM((slices, cells, cells), F32),
             pltpu.VMEM((ny, 2 * share, cells, cells), F32),
             pltpu.VMEM((ny, share, cells, cells), F32),
@@ -582,8 +516,6 @@
             dma((units, nz)), dma((units, nz)),
             dma((ny,)), dma((ny,)),
             dma((ny, 2)), dma((ny, 2)),
-            dma((chunks, groups, nz)), dma((chunks, groups, nz)),
-            dma((chunks, groups, nx)), dma((chunks, groups)),
             dma((nz,)), dma((nz,)),
             dma((nx,)), dma((nx,)),
             dma((2 * ny,)), dma((2 * ny,)),

time: 53.4 us -> 51.6 us (0.966)
  Pallas kernels: 52.7 us -> 50.9 us
    pallas_call x1, Pallas kernels: 51.9 us -> 50.1 us  [on_device(): pl.pallas_call(functools.partial(kernel, (nx, nz, ny, slices * nx * nz)),...]
where the time goes in v6:
time: 51.6 us; the launch traced here: 51.5 us
  Pallas kernels  50.9 us (99%)
  between operations  0.64 us (1%)
    pallas_call x1, Pallas kernels, on_device(): pl.pallas_call(functools.partial(kernel, (nx, nz, ny, slices * nx * nz)),...  50.1 us

profile of v6, /device:TPU:1, one launch (start us, length us, event | category | flops | bytes accessed | tf_op | source)
XLA Modules:
  0.0 51.5 jit_solution(5293226326944663624)
XLA Ops:
  0.6 50.1 %shard_map.86 = (f32[576,128]{1,0:T(8,128)S(1)}, f32[2,128,128]{2,1,0:T(8,128)S(1)}) custom-call(s32[2]{0:T(128)} %refs_0_.1, bf16[16,128,128]{2,1,0:T(8,128)(2,1)} %refs_1_.1, s32[16,192]{1,0:T(8,128)} %refs_2_.1, f32[16,192]{1,0:T(8,128)} %refs_3_.1, s32[16,192]{1,0:T(8,128)} %refs_4_.1, f32[16,192]{1,0:T(8,128)} %refs_5_.1, f32[576,128]{1,0:T(8,128)} %bitcast.10), custom_call_target="tpu_custom_call" | custom-call | tf_op jit(solution)/shard_map/pallas_call | solution.py:465
  50.7 0.8 %shard_map.87 = (f32[576,128]{1,0:T(8,128)}, f32[2,128,128]{2,1,0:T(8,128)}) custom-call(f32[576,128]{1,0:T(8,128)S(1)} %get-tuple-element.6.image, f32[2,128,128]{2,1,0:T(8,128)S(1)} %get-tuple-element.7.grad), custom_call_target="tpu_custom_call" | custom-call | tf_op jit(solution)/shard_map/pallas_call | solution.py:531

commit v7 on v6

--- a/solution.py
+++ b/solution.py
@@ -44,7 +44,7 @@
     share = slices // (2 * ny)
     groups = wide // 128
     last = chunks - 1
-    units = [(k, slice(0, groups)) for k in range(last)] + [(last, slice(0, 2)), (last, slice(2, groups))]
+    units = [(k, slice(0, groups)) for k in range(last)] + [(last, slice(0, groups))]
     depth, vw = lax.axis_index("depth"), lax.axis_index("views")
     x, z = depth // nz, depth % nz
     y, core = vw // 2, vw % 2

time: 51.6 us -> 51.2 us (level)
  no operation moved by 1% of the time
where the time goes in v7:
time: 51.2 us; the launch traced here: 51.1 us
  Pallas kernels  50.4 us (98%)
  between operations  0.64 us (1%)
    pallas_call x1, Pallas kernels, on_device(): pl.pallas_call(functools.partial(kernel, (nx, nz, ny, slices * nx * nz)),...  49.7 us

profile of v7, /device:TPU:1, one launch (start us, length us, event | category | flops | bytes accessed | tf_op | source)
XLA Modules:
  0.0 51.1 jit_solution(2646986625720733291)
XLA Ops:
  0.6 49.7 %shard_map.86 = (f32[576,128]{1,0:T(8,128)S(1)}, f32[2,128,128]{2,1,0:T(8,128)S(1)}) custom-call(s32[2]{0:T(128)} %refs_0_.1, bf16[16,128,128]{2,1,0:T(8,128)(2,1)} %refs_1_.1, s32[16,192]{1,0:T(8,128)} %refs_2_.1, f32[16,192]{1,0:T(8,128)} %refs_3_.1, s32[16,192]{1,0:T(8,128)} %refs_4_.1, f32[16,192]{1,0:T(8,128)} %refs_5_.1, f32[576,128]{1,0:T(8,128)} %bitcast.10), custom_call_target="tpu_custom_call" | custom-call | tf_op jit(solution)/shard_map/pallas_call | solution.py:465
  50.3 0.8 %shard_map.87 = (f32[576,128]{1,0:T(8,128)}, f32[2,128,128]{2,1,0:T(8,128)}) custom-call(f32[576,128]{1,0:T(8,128)S(1)} %get-tuple-element.6.image, f32[2,128,128]{2,1,0:T(8,128)S(1)} %get-tuple-element.7.grad), custom_call_target="tpu_custom_call" | custom-call | tf_op jit(solution)/shard_map/pallas_call | solution.py:531
